TPU v7x, 32 devices: a whole 2x2x4 slice. The times are simulated.
32 devices in a mesh: video: 2 (over y), rows: 4 (over z), cols: 4 (over x, core).
Axes of the slice: x: 2, y: 2, z: 4, core: 2. Of those that a mesh axis runs over, the one named last changes fastest.
Arguments:
- frame_in: bfloat16 [64, 80, 512], P(('video', 'rows'), 'cols'), parts along dimension 0, may hold values from -6 to 6
- norm_gain: float32 [512], replicated, may hold values from 0.5 to 1.5
- w_query: bfloat16 [512, 512], replicated, may hold values from -2 to 2
- w_key: bfloat16 [512, 512], replicated, may hold values from -0.125 to 0.125
- w_value: bfloat16 [512, 512], replicated, may hold values from -0.25 to 0.25
- w_out: bfloat16 [512, 512], replicated, may hold values from -0.25 to 0.25
- conv_gain: float32 [512], replicated, may hold values from 0.5 to 1.5
- conv_cache: bfloat16 [2, 64, 80, 512], P(None, ('video', 'rows'), 'cols'), parts along dimension 1, may hold values from -6 to 6
- w_conv: bfloat16 [3, 3, 3, 512, 256], replicated, may hold values from -0.0546875 to 0.0546875
- conv_bias: float32 [256], replicated, may hold values from -0.5 to 0.5
Outputs:
- hidden: bfloat16 [64, 80, 512], P(('video', 'rows'), 'cols'), parts along dimension 0
- mixed_out: bfloat16 [64, 80, 256], P(('video', 'rows'), 'cols'), parts along dimension 0
There are 2 independent parts, one for each index of `video`. A program takes and returns all parts, laid end to end along the dimension named above; an argument that names none is the same for every part. Nothing has to cross between parts.
All inputs are finite; a program needn't handle non-finite values.
Results may differ from a plain program's by a relative error of at most 0.012.
Values may be sent and summed in bfloat16 or wider, within the bound.
No kernel may reach another device: no remote copies, remote signals or barrier semaphores. Data moves between devices by JAX's collectives and lax.ppermute only.
A program may use at most 128 MiB of HBM per device.

v0:
```python
import math

import jax
import jax.numpy as jnp
from jax import lax
from jax.sharding import PartitionSpec as P


def padded_2(value, sides, width):
    for axis, dim in sides:
        size, length = (lax.axis_size(axis), value.shape[dim])
        up = [(i, (i + 1) % size) for i in range(size - 1)]
        down = [(j, i) for i, j in up]
        last = lax.slice_in_dim(value, length - width, length, axis=dim)
        first = lax.slice_in_dim(value, 0, width, axis=dim)
        before = lax.ppermute(last, axis, up)
        after = lax.ppermute(first, axis, down)
        value = jnp.concatenate([before, value, after], axis=dim)
    return value


def rms_scaled(values, gain):
    mean_sq = jnp.mean(values * values, axis=-1, keepdims=True)
    return values * lax.rsqrt(mean_sq + 1e-06) * gain


def fold_block(running_state, query_keys, block_rows):
    running, total_sum, accumulated = running_state
    scores = lax.dot_general(
        query_keys, block_rows, (((1,), (1,)), ((), ())), preferred_element_type=jnp.float32
    )
    new_max = jnp.maximum(running, jnp.max(scores, axis=1))
    weights = jnp.exp(scores - new_max[:, None])
    total_sum = jnp.sum(weights, axis=1)
    accumulated = jnp.dot(
        weights.astype(jnp.bfloat16), block_rows, preferred_element_type=jnp.float32
    )
    return (new_max, total_sum, accumulated)


def start_for(query_count, channels):
    return (
        jnp.full((query_count,), -1e30, jnp.float32),
        jnp.zeros((query_count,), jnp.float32),
        jnp.zeros((query_count, channels), jnp.float32),
    )


def body(
    frame_in, norm_gain, w_query, w_key, w_value, w_out, conv_gain, conv_cache, w_conv, conv_bias
):
    tile_rows, tile_cols, channels = frame_in.shape
    out_channels = w_conv.shape[4]
    count = tile_rows * tile_cols
    cache_padded = padded_2(conv_cache, (("rows", 1), ("cols", 2)), 1)
    tokens = frame_in.astype(jnp.float32).reshape(count, channels)
    normed = rms_scaled(tokens, norm_gain).astype(jnp.bfloat16)
    query_rows = (
        jnp.dot(normed, w_query, preferred_element_type=jnp.float32) * (1.0 / math.sqrt(channels))
    ).astype(jnp.bfloat16)
    query_keys = jnp.dot(query_rows, w_key.T, preferred_element_type=jnp.float32).astype(
        jnp.bfloat16
    )
    final_state = fold_block(
        start_for(count, channels),
        query_keys,
        lax.all_gather(normed, ("rows", "cols"), axis=0, tiled=True),
    )
    pooled = (final_state[2] / final_state[1][:, None]).astype(jnp.bfloat16)
    attended = jnp.dot(pooled, w_value, preferred_element_type=jnp.float32).astype(jnp.bfloat16)
    hidden = (tokens + jnp.dot(attended, w_out, preferred_element_type=jnp.float32)).astype(
        jnp.bfloat16
    )
    conv_input = jax.nn.silu(rms_scaled(hidden.astype(jnp.float32), conv_gain)).astype(jnp.bfloat16)
    conv_input = conv_input.reshape(1, tile_rows, tile_cols, channels)
    frame_padded = padded_2(conv_input, (("rows", 1), ("cols", 2)), 1)
    padded = jnp.concatenate([cache_padded, frame_padded], axis=0)
    windows = [
        padded[time_off, row_off : row_off + tile_rows, col_off : col_off + tile_cols, :]
        for time_off in range(3)
        for row_off in range(3)
        for col_off in range(3)
    ]
    patches = jnp.concatenate(windows, axis=-1).reshape(count, 27 * channels)
    kernel_rows = w_conv.reshape(27 * channels, out_channels)
    result_sum = hidden[:, :out_channels].astype(jnp.float32) + conv_bias
    result_sum = result_sum + jnp.dot(patches, kernel_rows, preferred_element_type=jnp.float32)
    hidden_out = hidden.reshape(tile_rows, tile_cols, channels)
    mixed_out = result_sum.astype(jnp.bfloat16).reshape(tile_rows, tile_cols, out_channels)
    return (hidden_out, mixed_out)


def solution(mesh):
    in_specs = (
        P(("video", "rows"), "cols", None),
        P(),
        P(),
        P(),
        P(),
        P(),
        P(),
        P(None, ("video", "rows"), "cols", None),
        P(),
        P(),
    )
    out_specs = (P(("video", "rows"), "cols", None), P(("video", "rows"), "cols", None))
    return jax.shard_map(body, mesh=mesh, in_specs=in_specs, out_specs=out_specs, check_vma=False)
```

profile of v0, /device:TPU:0, one launch (start us, length us, event | category | flops | bytes accessed | tf_op | source)
XLA Modules:
  0.0 100.9 jit_solution(12430634139479733988)
XLA Ops:
  7.2 1.1 %copy.97 = f32[8,20,512]{2,1,0:T(8,128)S(1)} copy(bf16[8,20,512]{2,0,1:T(8,128)(2,1)} %param.10) | data formatting | bytes 491520 | tf_op jit(solution)/shard_map/convert_element_type | solution.py:56
  8.3 1.0 %multiply_reduce_fusion = f32[8,20]{0,1:T(8,128)S(1)} fusion(bf16[8,20,512]{2,0,1:T(8,128)(2,1)} %param.10), kind=kLoop, calls=%fused_computation.32 | loop fusion | flops 245600 | bytes 164480 | tf_op jit(solution)/shard_map/reduce_sum | solution.py:23
  9.6 1.5 %multiply_convert_fusion = bf16[160,512]{1,0:T(8,128)(2,1)} fusion(f32[160,512]{1,0:T(8,128)S(1)} %reshape.106, f32[512]{0:T(512)} %param.11, f32[160]{0:T(256)S(1)} %rsqrt.20), kind=kLoop, calls=%fused_computation.31 | loop fusion | flops 245760 | bytes 494208 | tf_op jit(solution)/shard_map/convert_element_type | solution.py:57
  11.0 1.2 %fusion.28 = (bf16[2,1,20,512]{3,1,2,0:T(2,128)(2,1)S(1)}, bf16[2,1,20,512]{3,1,2,0:T(2,128)(2,1)S(1)}) fusion(bf16[2,8,20,512]{3,1,2,0:T(8,128)(2,1)} %param.17), kind=kLoop, calls=%fused_computation.90 | loop fusion | bytes 163840 | tf_op jit(solution)/shard_map/slice | solution.py:14
  12.2 1.3 %collective-permute-start.1 = (bf16[2,1,20,512]{3,1,2,0:T(2,128)(2,1)S(1)}, bf16[2,1,20,512]{3,1,2,0:T(2,128)(2,1)S(1)}, u32[]{:S(2)}, u32[]{:S(2)}) collective-permute-start(bf16[2,1,20,512]{3,1,2,0:T(2,128)(2,1)S(1)} %get-tuple-element.37), channel_id=1, source_target_pairs={{4,0},{8,4},{12,8},{5,1},{9,5},{13,9},{6,2},{10,6},{14,10},{7,3},{... | collective-permute-start | bytes 122888 | tf_op jit(solution)/shard_map/ppermute | solution.py:17
  13.5 5.6 %collective-permute-start = (bf16[2,1,20,512]{3,1,2,0:T(2,128)(2,1)S(1)}, bf16[2,1,20,512]{3,1,2,0:T(2,128)(2,1)S(1)}, u32[]{:S(2)}, u32[]{:S(2)}) collective-permute-start(bf16[2,1,20,512]{3,1,2,0:T(2,128)(2,1)S(1)} %get-tuple-element.36), channel_id=1, source_target_pairs={{0,4},{4,8},{8,12},{1,5},{5,9},{9,13},{2,6},{6,10},{10,14},{3,7},{... | collective-permute-start | bytes 122888 | tf_op jit(solution)/shard_map/ppermute | solution.py:16
  19.1 1.4 %fusion.2 = bf16[160,512]{1,0:T(8,128)(2,1)S(1)} fusion(bf16[160,512]{1,0:T(8,128)(2,1)} %multiply_convert_fusion, bf16[512,512]{1,0:T(8,128)(2,1)} %param.12), kind=kOutput, calls=%fused_computation.6 | convolution fusion | flops 84049920 | bytes 851968 | tf_op jit(solution)/shard_map/dot_general | solution.py:59
  20.5 1.0 %constant_dynamic-update-slice_fusion.1 = bf16[2,9,20,512]{3,1,2,0:T(8,128)(2,1)S(1)} fusion(bf16[2,8,20,512]{3,1,2,0:T(8,128)(2,1)} %param.17), kind=kLoop, calls=%fused_computation.49 | loop fusion | bytes 655360
  21.6 0.8 pad_maximum_fusion.7
  22.3 1.3 %collective-permute-start.3 = (bf16[2,10,1,512]{3,1,2,0:T(8,128)(2,1)S(1)}, bf16[2,10,1,512]{3,1,2,0:T(8,128)(2,1)S(1)}, u32[]{:S(2)}, u32[]{:S(2)}) collective-permute-start(bf16[2,10,1,512]{3,1,2,0:T(8,128)(2,1)S(1)} %get-tuple-element.28), channel_id=1, source_target_pairs={{1,0},{2,1},{3,2},{5,4},{6,5},{7,6},{9,8},{10,9},{11,10},{13,12},{... | collective-permute-start | bytes 61448 | tf_op jit(solution)/shard_map/ppermute | solution.py:17
  23.6 3.0 %collective-permute-start.2 = (bf16[2,10,1,512]{3,1,2,0:T(8,128)(2,1)S(1)}, bf16[2,10,1,512]{3,1,2,0:T(8,128)(2,1)S(1)}, u32[]{:S(2)}, u32[]{:S(2)}) collective-permute-start(bf16[2,10,1,512]{3,1,2,0:T(8,128)(2,1)S(1)} %get-tuple-element.29), channel_id=1, source_target_pairs={{0,1},{1,2},{2,3},{4,5},{5,6},{6,7},{8,9},{9,10},{10,11},{12,13},{... | collective-permute-start | bytes 61448 | tf_op jit(solution)/shard_map/ppermute | solution.py:16
  26.7 0.1 constant_dynamic-update-slice_fusion
  26.8 0.2 fusion.27
  27.8 0.6 pad_maximum_fusion
  28.4 1.2 %fusion.24 = (bf16[1,8,20,512]{3,1,2,0:T(8,128)(2,1)}, bf16[1,8,20,512]{3,1,2,0:T(8,128)(2,1)S(1)}, bf16[1,8,20,512]{3,1,2,0:T(8,128)(2,1)S(1)}, bf16[1,8,20,512...) fusion(bf16[2,10,21,512]{3,1,2,0:T(8,128)(2,1)S(1)} %get-tuple-, ...), kind=kLoop, calls=%fused_computation.86 | loop fusion | bytes 3932160 | tf_op jit(solution)/shard_map/slice | solution.py:79
  29.7 0.7 concatenate.106
  30.4 1.0 copy.101
  31.4 1.0 copy.102
  32.3 0.7 concatenate.111
  33.0 1.0 copy.104
  34.1 0.7 concatenate.114
  35.3 1.0 copy.114
  36.3 1.6 %constant_dynamic-update-slice_fusion.31 = bf16[160,13824]{1,0:T(8,128)(2,1)} fusion(bf16[160,512]{1,0:T(8,128)(2,1)} %concatenate.106), kind=kLoop, calls=%fused_computation.79 | loop fusion | bytes 327680
  38.0 0.7 constant_dynamic-update-slice_fusion.30
  38.7 0.7 constant_dynamic-update-slice_fusion.29
  39.3 1.6 %constant_dynamic-update-slice_fusion.28 = bf16[160,13824]{1,0:T(8,128)(2,1)} fusion(bf16[160,13824]{1,0:T(8,128)(2,1)} %constant_dynamic-update-slice_fusion.29, bf16[160,512]{1,0:T(8,128)(2,1)} %concatenate.111), kind=kLoop, calls=%fused_computation.76 | loop fusion | bytes 327680
  40.9 0.7 constant_dynamic-update-slice_fusion.27
  41.7 0.7 constant_dynamic-update-slice_fusion.26
  42.4 1.6 %constant_dynamic-update-slice_fusion.25 = bf16[160,13824]{1,0:T(8,128)(2,1)} fusion(bf16[160,13824]{1,0:T(8,128)(2,1)} %constant_dynamic-update-slice_fusion.26, bf16[160,512]{1,0:T(8,128)(2,1)} %concatenate.114), kind=kLoop, calls=%fused_computation.73 | loop fusion | bytes 327680
  43.9 0.7 constant_dynamic-update-slice_fusion.24
  44.7 0.7 constant_dynamic-update-slice_fusion.23
  45.4 0.7 constant_dynamic-update-slice_fusion.22
  46.1 0.7 constant_dynamic-update-slice_fusion.21
  46.8 0.7 constant_dynamic-update-slice_fusion.20
  47.5 0.7 constant_dynamic-update-slice_fusion.19
  48.2 0.7 constant_dynamic-update-slice_fusion.18
  48.9 0.7 constant_dynamic-update-slice_fusion.17
  49.5 0.7 constant_dynamic-update-slice_fusion.16
  50.2 6.4 %all-gather.2.cloned.1.call-done = bf16[2560,512]{1,0:T(8,128)(2,1)} async-done(((bf16[160,512]{1,0:T(8,128)(2,1)}), bf16[2560,512]{1,0:T(8,128)(2,1)}) %all-gather.2.cloned.1.call-update) | async-done | bytes 2621456 | tf_op jit(solution)/shard_map/all_gather | solution.py:67
  56.6 3.1 %fusion.31 = (f32[160]{0:T(256)S(1)}, f32[160,2560]{1,0:T(8,128)S(1)}) fusion(bf16[2560,512]{1,0:T(8,128)(2,1)} %all-gather.2.cloned.1.call-done, bf16[160,512]{1,0:T(8,128)(2,1)S(1)} %fusion.2, bf16[512,512]{1,0:T(8,128)(2,1)S(1)} %copy-done), kind=kOutput, calls=%fused_computation.93 | convolution fusion | flops 503807840 | bytes 4948608 | tf_op jit(solution)/shard_map/dot_general | solution.py:29
  59.8 0.4 fusion
  60.1 3.3 %convolution_convert_fusion = bf16[160,512]{1,0:T(8,128)(2,1)} fusion(bf16[512,512]{1,0:T(8,128)(2,1)} %param.14, bf16[2560,512]{1,0:T(8,128)(2,1)} %all-gather.2.cloned.1.call-done, f32[160,2560]{1,0:T(8,128)S(1)} %get-tuple-element.55, f32[160]{0:T(256)S(1)} %broadcast_maximum_fusion, f32[160]{0:T(256)S(1)} %fusion), kind=kOutput, calls=%fused_computation.8 | convolution fusion | flops 504381440 | bytes 4949248 | tf_op jit(solution)/shard_map/dot_general | solution.py:70
  63.5 1.3 %fusion.11 = (f32[160]{0:T(256)S(1)}, bf16[160,512]{1,0:T(8,128)(2,1)S(1)}) fusion(f32[160,512]{1,0:T(8,128)S(1)} %reshape.106, bf16[160,512]{1,0:T(8,128)(2,1)} %convolution_convert_fusion, bf16[512,512]{1,0:T(8,128)(2,1)S(1)} %copy-done.3), kind=kOutput, calls=%fused_computation.23 | convolution fusion | flops 84295520 | bytes 1180288 | tf_op jit(solution)/shard_map/dot_general | solution.py:71
  64.8 0.2 fusion.18
  65.0 3.1 %collective-permute-start.4 = (bf16[1,1,20,512]{3,2,1,0:T(8,128)(2,1)S(1)}, bf16[1,1,20,512]{3,2,1,0:T(8,128)(2,1)S(1)}, u32[]{:S(2)}, u32[]{:S(2)}) collective-permute-start(bf16[1,1,20,512]{3,2,1,0:T(8,128)(2,1)S(1)} %get-tuple-element.53), channel_id=1, source_target_pairs={{0,4},{4,8},{8,12},{1,5},{5,9},{9,13},{2,6},{6,10},{10,14},{3,7},{... | collective-permute-start | bytes 61448 | tf_op jit(solution)/shard_map/ppermute | solution.py:16
  68.1 0.7 constant_dynamic-update-slice_fusion.15
  69.0 1.3 %collective-permute-start.5 = (bf16[1,1,20,512]{3,2,1,0:T(8,128)(2,1)S(1)}, bf16[1,1,20,512]{3,2,1,0:T(8,128)(2,1)S(1)}, u32[]{:S(2)}, u32[]{:S(2)}) collective-permute-start(bf16[1,1,20,512]{3,2,1,0:T(8,128)(2,1)S(1)} %get-tuple-element.52), channel_id=1, source_target_pairs={{4,0},{8,4},{12,8},{5,1},{9,5},{13,9},{6,2},{10,6},{14,10},{7,3},{... | collective-permute-start | bytes 61448 | tf_op jit(solution)/shard_map/ppermute | solution.py:17
  70.3 4.4 %collective-permute-done.5 = bf16[1,1,20,512]{3,2,1,0:T(8,128)(2,1)S(1)} collective-permute-done((bf16[1,1,20,512]{3,2,1,0:T(8,128)(2,1)S(1)}, bf16[1,1,20,512]{3,2,1,0:T(8,128)(2,1)S(1)}, u32[]{:S(2)}, u32[]{:S(2)}) %collective-permute-start.5) | collective-permute-done | bytes 20512 | tf_op jit(solution)/shard_map/ppermute | solution.py:17
  74.8 1.3 %collective-permute-start.7 = (bf16[1,10,1,512]{3,2,1,0:T(2,128)(2,1)S(1)}, bf16[1,10,1,512]{3,2,1,0:T(2,128)(2,1)S(1)}, u32[]{:S(2)}, u32[]{:S(2)}) collective-permute-start(bf16[1,10,1,512]{3,2,1,0:T(2,128)(2,1)S(1)} %get-tuple-element.47), channel_id=1, source_target_pairs={{1,0},{2,1},{3,2},{5,4},{6,5},{7,6},{9,8},{10,9},{11,10},{13,12},{... | collective-permute-start | bytes 30728 | tf_op jit(solution)/shard_map/ppermute | solution.py:17
  76.1 3.0 %collective-permute-start.6 = (bf16[1,10,1,512]{3,2,1,0:T(2,128)(2,1)S(1)}, bf16[1,10,1,512]{3,2,1,0:T(2,128)(2,1)S(1)}, u32[]{:S(2)}, u32[]{:S(2)}) collective-permute-start(bf16[1,10,1,512]{3,2,1,0:T(2,128)(2,1)S(1)} %get-tuple-element.48), channel_id=1, source_target_pairs={{0,1},{1,2},{2,3},{4,5},{5,6},{6,7},{8,9},{9,10},{10,11},{12,13},{... | collective-permute-start | bytes 30728 | tf_op jit(solution)/shard_map/ppermute | solution.py:16
  79.1 0.7 constant_dynamic-update-slice_fusion.14
  79.9 0.7 copy.117
  80.7 0.3 pad_maximum_fusion.1
  81.1 0.7 constant_dynamic-update-slice_fusion.13
  81.8 0.7 constant_dynamic-update-slice_fusion.12
  82.5 0.7 constant_dynamic-update-slice_fusion.11
  83.2 0.7 constant_dynamic-update-slice_fusion.10
  83.9 0.9 constant_dynamic-update-slice_fusion.9
  84.9 0.7 constant_dynamic-update-slice_fusion.8
  85.6 0.7 constant_dynamic-update-slice_fusion.7
  86.3 0.7 constant_dynamic-update-slice_fusion.6
  87.0 0.7 constant_dynamic-update-slice_fusion.5
  87.7 5.7 %fusion.6 = bf16[160,256]{1,0:T(8,128)(2,1)S(1)} fusion(bf16[160,13824]{1,0:T(8,128)(2,1)} %constant_dynamic-update-slice_fusion.5, bf16[13824,256]{1,0:T(8,128)(2,1)} %bitcast.12, bf16[160,512]{1,0:T(8,128)(2,1)S(1)} %get-tuple-element.57, f32[256]{0:T(256)S(1)} %copy-done.5), kind=kOutput, calls=%fused_computation.13 | convolution fusion | flops 1132625920 | bytes 11666432 | tf_op jit(solution)/shard_map/dot_general | solution.py:87
  93.4 0.7 copy.118
  (73 shorter events, 2.2 us)
Async XLA Ops:
  7.2 49.5 %copy-start = (bf16[512,512]{1,0:T(8,128)(2,1)S(1)}, bf16[512,512]{1,0:T(8,128)(2,1)}, u32[]{:S(2)}) copy-start(bf16[512,512]{1,0:T(8,128)(2,1)} %param.13) | copy-start | bytes 1572868
  7.2 19.7 %copy-start.1 = (bf16[2,8,20,512]{3,1,2,0:T(8,128)(2,1)S(1)}, bf16[2,8,20,512]{3,1,2,0:T(8,128)(2,1)}, u32[]{:S(2)}) copy-start(bf16[2,8,20,512]{3,1,2,0:T(8,128)(2,1)} %param.17) | copy-start | bytes 983044
  7.2 49.5 %all-gather.2.cloned.1.call-start = ((), (), s32[]{:S(2)}) async-start(), calls=%async_computation | async-start | bytes 2785280 | tf_op jit(solution)/shard_map/all_gather | solution.py:67
  12.2 9.3 %collective-permute-start.1 = (bf16[2,1,20,512]{3,1,2,0:T(2,128)(2,1)S(1)}, bf16[2,1,20,512]{3,1,2,0:T(2,128)(2,1)S(1)}, u32[]{:S(2)}, u32[]{:S(2)}) collective-permute-start(bf16[2,1,20,512]{3,1,2,0:T(2,128)(2,1)S(1)} %get-tuple-element.37), channel_id=1, source_target_pairs={{4,0},{8,4},{12,8},{5,1},{9,5},{13,9},{6,2},{10,6},{14,10},{7,3},{... | collective-permute-start | bytes 122888 | tf_op jit(solution)/shard_map/ppermute | solution.py:17
  13.5 8.0 %collective-permute-start = (bf16[2,1,20,512]{3,1,2,0:T(2,128)(2,1)S(1)}, bf16[2,1,20,512]{3,1,2,0:T(2,128)(2,1)S(1)}, u32[]{:S(2)}, u32[]{:S(2)}) collective-permute-start(bf16[2,1,20,512]{3,1,2,0:T(2,128)(2,1)S(1)} %get-tuple-element.36), channel_id=1, source_target_pairs={{0,4},{4,8},{8,12},{1,5},{5,9},{9,13},{2,6},{6,10},{10,14},{3,7},{... | collective-permute-start | bytes 122888 | tf_op jit(solution)/shard_map/ppermute | solution.py:16
  22.3 5.4 %collective-permute-start.3 = (bf16[2,10,1,512]{3,1,2,0:T(8,128)(2,1)S(1)}, bf16[2,10,1,512]{3,1,2,0:T(8,128)(2,1)S(1)}, u32[]{:S(2)}, u32[]{:S(2)}) collective-permute-start(bf16[2,10,1,512]{3,1,2,0:T(8,128)(2,1)S(1)} %get-tuple-element.28), channel_id=1, source_target_pairs={{1,0},{2,1},{3,2},{5,4},{6,5},{7,6},{9,8},{10,9},{11,10},{13,12},{... | collective-permute-start | bytes 61448 | tf_op jit(solution)/shard_map/ppermute | solution.py:17
  23.6 4.1 %collective-permute-start.2 = (bf16[2,10,1,512]{3,1,2,0:T(8,128)(2,1)S(1)}, bf16[2,10,1,512]{3,1,2,0:T(8,128)(2,1)S(1)}, u32[]{:S(2)}, u32[]{:S(2)}) collective-permute-start(bf16[2,10,1,512]{3,1,2,0:T(8,128)(2,1)S(1)} %get-tuple-element.29), channel_id=1, source_target_pairs={{0,1},{1,2},{2,3},{4,5},{5,6},{6,7},{8,9},{9,10},{10,11},{12,13},{... | collective-permute-start | bytes 61448 | tf_op jit(solution)/shard_map/ppermute | solution.py:16
  59.7 3.8 %copy-start.3 = (bf16[512,512]{1,0:T(8,128)(2,1)S(1)}, bf16[512,512]{1,0:T(8,128)(2,1)}, u32[]{:S(2)}) copy-start(bf16[512,512]{1,0:T(8,128)(2,1)} %param.15) | copy-start | bytes 1572868
  59.7 5.0 %copy-start.4 = (f32[512]{0:T(512)S(1)}, f32[512]{0:T(512)}, u32[]{:S(2)}) copy-start(f32[512]{0:T(512)} %param.16) | copy-start | bytes 6148
  59.7 9.1 %copy-start.2 = (bf16[1,8,20,512]{3,1,2,0:T(8,128)(2,1)S(1)}, bf16[1,8,20,512]{3,1,2,0:T(8,128)(2,1)}, u32[]{:S(2)}) copy-start(bf16[1,8,20,512]{3,1,2,0:T(8,128)(2,1)} %get-tuple-element.12) | copy-start | bytes 491524
  65.0 5.3 %collective-permute-start.4 = (bf16[1,1,20,512]{3,2,1,0:T(8,128)(2,1)S(1)}, bf16[1,1,20,512]{3,2,1,0:T(8,128)(2,1)S(1)}, u32[]{:S(2)}, u32[]{:S(2)}) collective-permute-start(bf16[1,1,20,512]{3,2,1,0:T(8,128)(2,1)S(1)} %get-tuple-element.53), channel_id=1, source_target_pairs={{0,4},{4,8},{8,12},{1,5},{5,9},{9,13},{2,6},{6,10},{10,14},{3,7},{... | collective-permute-start | bytes 61448 | tf_op jit(solution)/shard_map/ppermute | solution.py:16
  69.0 5.7 %collective-permute-start.5 = (bf16[1,1,20,512]{3,2,1,0:T(8,128)(2,1)S(1)}, bf16[1,1,20,512]{3,2,1,0:T(8,128)(2,1)S(1)}, u32[]{:S(2)}, u32[]{:S(2)}) collective-permute-start(bf16[1,1,20,512]{3,2,1,0:T(8,128)(2,1)S(1)} %get-tuple-element.52), channel_id=1, source_target_pairs={{4,0},{8,4},{12,8},{5,1},{9,5},{13,9},{6,2},{10,6},{14,10},{7,3},{... | collective-permute-start | bytes 61448 | tf_op jit(solution)/shard_map/ppermute | solution.py:17
  74.7 12.9 %copy-start.5 = (f32[256]{0:T(256)S(1)}, f32[256]{0:T(256)}, u32[]{:S(2)}) copy-start(f32[256]{0:T(256)} %param.19) | copy-start | bytes 3076
  74.8 5.9 %collective-permute-start.7 = (bf16[1,10,1,512]{3,2,1,0:T(2,128)(2,1)S(1)}, bf16[1,10,1,512]{3,2,1,0:T(2,128)(2,1)S(1)}, u32[]{:S(2)}, u32[]{:S(2)}) collective-permute-start(bf16[1,10,1,512]{3,2,1,0:T(2,128)(2,1)S(1)} %get-tuple-element.47), channel_id=1, source_target_pairs={{1,0},{2,1},{3,2},{5,4},{6,5},{7,6},{9,8},{10,9},{11,10},{13,12},{... | collective-permute-start | bytes 30728 | tf_op jit(solution)/shard_map/ppermute | solution.py:17
  76.1 4.6 %collective-permute-start.6 = (bf16[1,10,1,512]{3,2,1,0:T(2,128)(2,1)S(1)}, bf16[1,10,1,512]{3,2,1,0:T(2,128)(2,1)S(1)}, u32[]{:S(2)}, u32[]{:S(2)}) collective-permute-start(bf16[1,10,1,512]{3,2,1,0:T(2,128)(2,1)S(1)} %get-tuple-element.48), channel_id=1, source_target_pairs={{0,1},{1,2},{2,3},{4,5},{5,6},{6,7},{8,9},{9,10},{10,11},{12,13},{... | collective-permute-start | bytes 30728 | tf_op jit(solution)/shard_map/ppermute | solution.py:16
Sparse Core Ops, SparseCore 0:
  11.1 45.4 all-gather.1
where the time goes:
time: 102 us; the launch traced here: 101 us
  local copies, waits for them, and re-layouts  34.8 us (34%)
  starting transfers between devices  20 us (20%)
  matrix products  14.7 us (14%)
  between operations  14.7 us (14%)
  waiting for transfers between devices  10.8 us (11%)
  other arithmetic  5.83 us (6%)
    unnamed x41, local copies, waits for them, and re-layouts  22.5 us
    ppermute x4, starting transfers between devices, padded_2(): before = lax.ppermute(last, axis, up)  14.8 us
    all_gather x1, waiting for transfers between devices, body(): lax.all_gather(normed, ('rows', 'cols'), axis=0, tiled=True)  6.41 us
    slice x20, local copies, waits for them, and re-layouts, body(): padded[time_off, row_off:row_off + tile_rows, col_off:col_off + tile_cols...  5.93 us
    dot_general x1, matrix products, body(): jnp.dot(patches, kernel_rows, preferred_element_type=jnp.float32)  5.69 us
    ppermute x4, starting transfers between devices, padded_2(): after = lax.ppermute(first, axis, down)  5.17 us
    ppermute x4, waiting for transfers between devices, padded_2(): after = lax.ppermute(first, axis, down)  4.41 us
    concatenate x27, local copies, waits for them, and re-layouts, body(): patches = jnp.concatenate(windows, axis=-1).reshape(count, 27 * channels)  3.61 us
  transfers between devices with their start and end apart: 9, of which 2 were waited for; matrix products, arithmetic and copies ran while one was open for 30% of the time, Pallas kernels for 0%

commit v1 on v0

v1 whole, which is shorter than its diff:
```python
import functools
import math

import jax
import jax.numpy as jnp
from jax import lax
from jax.experimental import pallas as pl
from jax.experimental.pallas import tpu as pltpu
from jax.sharding import PartitionSpec as P

EPS = 1e-06
AXES = ("rows", "cols")
F32 = jnp.float32
BF16 = jnp.bfloat16
VM = pl.BlockSpec(memory_space=pltpu.VMEM)


def chip_cycle(height, width):
    if width == 1 or height == 1:
        return [(z, x) for z in range(height) for x in range(width)]
    order = []
    for x in range(width):
        inner = range(1, height) if x % 2 == 0 else range(height - 1, 0, -1)
        order += [(z, x) for z in inner]
    return order + [(0, x) for x in range(width - 1, -1, -1)]


def permutations(rows, cols):
    def at(z, x, core):
        return z * cols + 2 * x + core

    walk = chip_cycle(rows, cols // 2)
    ring = []
    for k, here in enumerate(walk):
        there = walk[(k + 1) % len(walk)]
        ring += [(at(*here, 0), at(*there, 0)), (at(*there, 1), at(*here, 1))]
    twin = [(i, i ^ 1) for i in range(rows * cols)]
    down = [(i, i + cols) for i in range((rows - 1) * cols)]
    up = [(j, i) for i, j in down]
    cross = []
    for r in range(rows):
        for c in range(1, cols - 1, 2):
            i = r * cols + c
            cross += [(i, i + 1), (i + 1, i)]
    return len(walk), ring, twin, down, up, cross


def edge_slots(width):
    return -(-(width + 2) // 16) * 16


def side_slots(height):
    return height + 8


def rms_scaled(values, gain):
    mean_sq = jnp.mean(values * values, axis=-1, keepdims=True)
    return values * lax.rsqrt(mean_sq + EPS) * gain


def dot(a, b):
    return jnp.dot(a, b, preferred_element_type=F32)


def dot_t(a, b):
    return lax.dot_general(a, b, (((1,), (1,)), ((), ())), preferred_element_type=F32)


def pack_rows_kernel(frame_ref, cache_ref, first_ref, last_ref):
    width, height, channels = frame_ref.shape
    fill = jnp.zeros((edge_slots(width) - width, channels), F32)
    for t in range(3):
        tile = (frame_ref[...] if t == 2 else cache_ref[t]).astype(F32)
        for r, out in ((0, first_ref), (height - 1, last_ref)):
            row = jnp.concatenate([tile[c, r : r + 1, :] for c in range(width)] + [fill], axis=0)
            out[t] = row.astype(BF16)


def pack_cols_kernel(frame_ref, cache_ref, top_ref, bottom_ref, twin_ref, cross_ref):
    width, height, channels = frame_ref.shape
    odd = lax.rem(lax.axis_index("cols"), 2)
    fill = jnp.zeros((side_slots(height) - height - 2, channels), F32)
    for t in range(3):
        sides = []
        for c in (0, width - 1):
            own = (frame_ref[c] if t == 2 else cache_ref[t, c]).astype(F32)
            top = top_ref[t].astype(F32)[c : c + 1, :]
            bottom = bottom_ref[t].astype(F32)[c : c + 1, :]
            sides.append(jnp.concatenate([own, top, bottom, fill], axis=0))
        left, right = sides
        twin_ref[t] = jnp.where(odd == 1, left, right).astype(BF16)
        cross_ref[t] = jnp.where(odd == 1, right, left).astype(BF16)


def extended(own, top, bottom, twin, cross, odd):
    height = twin.shape[0] - side_slots(0)
    left = jnp.where(odd == 1, twin, cross)
    right = jnp.where(odd == 1, cross, twin)
    slot = lax.broadcasted_iota(jnp.int32, top.shape, 0)
    width = own.shape[0] // height

    def edge(row, k):
        row = jnp.where(slot == width, right[k : k + 1, :], row)
        return jnp.where(slot == top.shape[0] - 1, left[k : k + 1, :], row)

    return jnp.concatenate(
        [edge(top, height), left[:height], own, right[:height], edge(bottom, height + 1)], axis=0
    )


def conv_rows(ext_len, slots, i):
    return (0 if i == 0 else slots), (ext_len if i == 2 else ext_len - slots)


def add_taps(sums, products, i, j, height, count):
    slots = edge_slots(count // height)
    main = products[slots:] if i == 0 else products
    part = main[j * height : j * height + count]
    edge = None
    if i == 0:
        edge = products[:slots]
    if i == 2:
        edge = products[products.shape[0] - slots :]
    if edge is not None and j != 1:
        edge = pltpu.roll(edge, 1 if j == 0 else slots - 1, 0)
    if sums is None:
        return part, edge
    return sums[0] + part, (None if edge is None else sums[1] + edge)


def shifted_rows(sums, i, height):
    main, edge = sums
    if i == 1:
        return main
    count, out = main.shape
    width = count // height
    tile = main.reshape(width, height, out)
    moved = pltpu.roll(tile, 1 if i == 0 else height - 1, 1)
    row = lax.broadcasted_iota(jnp.int32, (height, out), 0)
    at = 0 if i == 0 else height - 1
    cells = [jnp.where(row == at, edge[c : c + 1, :], moved[c]) for c in range(width)]
    return jnp.concatenate(cells, axis=0)


def cache_conv_kernel(cache_ref, top_ref, bottom_ref, twin_ref, cross_ref, w_ref, out_ref, ext, acc):
    step = pl.program_id(0)
    width, height, channels = cache_ref.shape[1:]
    count = width * height
    odd = lax.rem(lax.axis_index("cols"), 2)

    @pl.when(step == 0)
    def _():
        for t in range(2):
            tokens = extended(
                cache_ref[t].reshape(count, channels).astype(F32),
                top_ref[t].astype(F32),
                bottom_ref[t].astype(F32),
                twin_ref[t].astype(F32),
                cross_ref[t].astype(F32),
                odd,
            )
            ext[t] = tokens.astype(BF16)

    ext_len = ext.shape[1]
    for i in range(3):

        @pl.when(step == i)
        def _():
            lo, hi = conv_rows(ext_len, top_ref.shape[1], i)
            sums = None
            for j in range(3):
                products = dot(ext[0, lo:hi, :], w_ref[0, 0, j]) + dot(ext[1, lo:hi, :], w_ref[1, 0, j])
                sums = add_taps(sums, products, i, j, height, count)
            value = shifted_rows(sums, i, height)
            if i == 0:
                acc[...] = value
            elif i == 1:
                acc[...] += value
            else:
                out_ref[...] = acc[...] + value


def cache_conv(cache, top, bottom, twin, cross, w_conv):
    _, width, height, channels = cache.shape
    out = w_conv.shape[4]
    ext_len = 2 * top.shape[1] + (width + 2) * height

    def whole(shape):
        return pl.BlockSpec(shape, lambda s: (0,) * len(shape))

    return pl.pallas_call(
        cache_conv_kernel,
        grid=(3,),
        in_specs=[
            whole(cache.shape),
            whole(top.shape),
            whole(bottom.shape),
            whole(twin.shape),
            whole(cross.shape),
            pl.BlockSpec((2, 1, 3, channels, out), lambda s: (0, s, 0, 0, 0)),
        ],
        out_specs=pl.BlockSpec((width * height, out), lambda s: (0, 0)),
        out_shape=jax.ShapeDtypeStruct((width * height, out), F32),
        scratch_shapes=[
            pltpu.VMEM((2, ext_len, channels), BF16),
            pltpu.VMEM((width * height, out), F32),
        ],
        name="cache_conv",
    )(cache, top, bottom, twin, cross, w_conv)


def query_kernel(frame_ref, top_ref, bottom_ref, twin_ref, cross_ref, gain_ref, wq_ref, wk_ref, raw_ref, keys_ref):
    width, height, channels = frame_ref.shape
    odd = lax.rem(lax.axis_index("cols"), 2)
    tokens = extended(
        frame_ref[...].reshape(width * height, channels).astype(F32),
        top_ref[...].astype(F32),
        bottom_ref[...].astype(F32),
        twin_ref[...].astype(F32),
        cross_ref[...].astype(F32),
        odd,
    )
    raw_ref[...] = tokens.astype(BF16)
    normed = rms_scaled(tokens, gain_ref[...]).astype(BF16)
    rows = (dot(normed, wq_ref[...]) * (1.0 / math.sqrt(channels))).astype(BF16)
    keys_ref[...] = dot_t(rows, wk_ref[...]).astype(BF16)


def lanes(value, width):
    return jnp.broadcast_to(value, (value.shape[0], width))


def fold_kernel(blocks, first, *refs):
    gain_ref, own_ref, twin_ref = refs[:3]
    block_refs = refs[3 : 3 + blocks]
    refs = refs[3 + blocks :]
    states, outs = ((None, None), refs) if first else (refs[:2], refs[2:])
    gain = gain_ref[...]
    keys = jnp.concatenate(
        [rms_scaled(b[...].astype(F32), gain).astype(BF16) for b in block_refs], axis=0
    )
    channels = keys.shape[1]
    for query_ref, state, out in zip((own_ref, twin_ref), states, outs):
        scores = dot_t(query_ref[...], keys)
        peak = jnp.max(scores, axis=1, keepdims=True)
        if not first:
            before = state[:, channels : channels + 1]
            peak = jnp.maximum(peak, before)
        weights = jnp.exp(scores - peak)
        total = jnp.sum(weights, axis=1, keepdims=True)
        summed = dot(weights.astype(BF16), keys)
        if not first:
            fade = jnp.exp(before - peak)
            total = total + fade * state[:, channels + 128 : channels + 129]
            summed = summed + fade * state[:, :channels]
        out[:, :channels] = summed
        out[:, channels : channels + 128] = lanes(peak, 128)
        out[:, channels + 128 :] = lanes(total, 128)


def fold(states, own, twin, gain, blocks):
    length, channels = own.shape
    shape = jax.ShapeDtypeStruct((length, channels + 256), F32)
    first = states is None
    return pl.pallas_call(
        functools.partial(fold_kernel, len(blocks), first),
        in_specs=[VM] * (3 + len(blocks) + (0 if first else 2)),
        out_specs=[VM, VM],
        out_shape=[shape, shape],
        name="fold",
    )(gain, own, twin, *blocks, *(() if first else states))


def finish_kernel(
    height, state_ref, other_ref, raw_ref, wv_ref, wo_ref, gain_ref, bias_ref, partial_ref, w_ref,
    hidden_ref, mixed_ref, w_buf, sem,
):
    fetch = pltpu.make_async_copy(w_ref.at[2], w_buf, sem)
    fetch.start()
    length, channels = raw_ref.shape
    count, out = partial_ref.shape
    slots = edge_slots(count // height)
    row = lax.axis_index("rows")
    col = lax.axis_index("cols")
    has_top, has_bottom = row > 0, row < lax.axis_size("rows") - 1
    has_left, has_right = col > 0, col < lax.axis_size("cols") - 1

    peak_a, peak_b = state_ref[:, channels : channels + 1], other_ref[:, channels : channels + 1]
    peak = jnp.maximum(peak_a, peak_b)
    fade_a, fade_b = jnp.exp(peak_a - peak), jnp.exp(peak_b - peak)
    total = fade_a * state_ref[:, channels + 128 : channels + 129]
    total = total + fade_b * other_ref[:, channels + 128 : channels + 129]
    summed = fade_a * state_ref[:, :channels] + fade_b * other_ref[:, :channels]
    pooled = (summed / total).astype(BF16)
    attended = dot(pooled, wv_ref[...]).astype(BF16)
    hidden = (raw_ref[...].astype(F32) + dot(attended, wo_ref[...])).astype(BF16)
    wide = hidden.astype(F32)
    value = rms_scaled(wide, gain_ref[...])
    value = value / (1.0 + jnp.exp(-value))
    slot = lax.broadcasted_iota(jnp.int32, (length, 1), 0)
    main_end = length - slots
    width = count // height
    in_top, in_bottom = slot < slots, slot >= main_end
    in_left = (slot >= slots) & (slot < slots + height)
    in_right = (slot >= main_end - height) & (slot < main_end)
    in_left = in_left | (slot == slots - 1) | (slot == length - 1)
    in_right = in_right | (slot == width) | (slot == main_end + width)
    outside = (in_top & jnp.logical_not(has_top)) | (in_bottom & jnp.logical_not(has_bottom))
    outside = outside | (in_left & jnp.logical_not(has_left)) | (in_right & jnp.logical_not(has_right))
    ext = jnp.where(outside, 0.0, value).astype(BF16)

    own = hidden[slots + height : slots + height + count]
    hidden_ref[...] = own
    result = partial_ref[...] + own[:, :out].astype(F32) + bias_ref[...]
    fetch.wait()
    for i in range(3):
        lo, hi = conv_rows(length, slots, i)
        sums = None
        for j in range(3):
            sums = add_taps(sums, dot(ext[lo:hi], w_buf[i, j]), i, j, height, count)
        result = result + shifted_rows(sums, i, height)
    mixed_ref[...] = result.astype(BF16)


def finish(height, state, other, raw, w_value, w_out, gain, bias, partial, w_conv):
    count, out = partial.shape
    channels = raw.shape[1]
    return pl.pallas_call(
        functools.partial(finish_kernel, height),
        in_specs=[VM] * 8 + [pl.BlockSpec(memory_space=pl.ANY)],
        out_specs=[VM, VM],
        out_shape=[
            jax.ShapeDtypeStruct((count, channels), BF16),
            jax.ShapeDtypeStruct((count, out), BF16),
        ],
        scratch_shapes=[pltpu.VMEM(w_conv.shape[1:], BF16), pltpu.SemaphoreType.DMA],
        name="finish",
    )(state, other, raw, w_value, w_out, gain, bias, partial, w_conv)


def body(
    frame_in, norm_gain, w_query, w_key, w_value, w_out, conv_gain, conv_cache, w_conv, conv_bias
):
    height, width, channels = frame_in.shape
    out_channels = w_conv.shape[4]
    count = height * width
    chips, ring, twin_pairs, down, up, cross_pairs = permutations(
        lax.axis_size("rows"), lax.axis_size("cols")
    )
    frame = jnp.transpose(frame_in, (1, 0, 2))
    cache = jnp.transpose(conv_cache, (0, 2, 1, 3))
    own = frame.reshape(count, channels)
    gain = norm_gain.reshape(1, channels)

    chain_a = own
    chain_b = lax.ppermute(own, AXES, twin_pairs)
    blocks = [[own]]
    hops = chips // 2
    for hop in range(hops):
        chain_a = lax.ppermute(chain_a, AXES, ring)
        arrived = [chain_a]
        if hop < hops - 1 or chips % 2:
            chain_b = lax.ppermute(chain_b, AXES, ring)
            arrived.append(chain_b)
        blocks.append(arrived)

    edge = jax.ShapeDtypeStruct((3, edge_slots(width), channels), BF16)
    first, last = pl.pallas_call(
        pack_rows_kernel, in_specs=[VM, VM], out_specs=[VM, VM], out_shape=[edge, edge], name="pack_rows"
    )(frame, cache)
    top = lax.ppermute(last, AXES, down)
    bottom = lax.ppermute(first, AXES, up)
    side = jax.ShapeDtypeStruct((3, side_slots(height), channels), BF16)
    to_twin, to_cross = pl.pallas_call(
        pack_cols_kernel, in_specs=[VM] * 4, out_specs=[VM, VM], out_shape=[side, side], name="pack_cols"
    )(frame, cache, top, bottom)
    twin = lax.ppermute(to_twin, AXES, twin_pairs)
    cross = lax.ppermute(to_cross, AXES, cross_pairs)

    length = 2 * edge_slots(width) + (width + 2) * height
    ext_shape = jax.ShapeDtypeStruct((length, channels), BF16)
    raw, queries = pl.pallas_call(
        query_kernel, in_specs=[VM] * 8, out_specs=[VM, VM], out_shape=[ext_shape, ext_shape], name="query"
    )(frame, top[2], bottom[2], twin[2], cross[2], gain, w_query, w_key)
    twin_queries = lax.ppermute(queries, AXES, twin_pairs)
    partial = cache_conv(cache, top, bottom, twin, cross, w_conv)

    groups, waiting = [], []
    for hop, arrived in enumerate(blocks):
        waiting = waiting + arrived
        if hop >= len(blocks) - 2 or len(waiting) >= 5:
            groups.append(waiting)
            waiting = []
    states = None
    for group in groups:
        states = fold(states, queries, twin_queries, gain, group)
    other = lax.ppermute(states[1], AXES, twin_pairs)
    hidden, mixed = finish(
        height, states[0], other, raw, w_value, w_out, conv_gain.reshape(1, channels),
        conv_bias.reshape(1, out_channels), partial, w_conv,
    )
    hidden = jnp.transpose(hidden.reshape(width, height, channels), (1, 0, 2))
    mixed = jnp.transpose(mixed.reshape(width, height, out_channels), (1, 0, 2))
    return (hidden, mixed)


def solution(mesh):
    in_specs = (
        P(("video", "rows"), "cols", None),
        P(),
        P(),
        P(),
        P(),
        P(),
        P(),
        P(None, ("video", "rows"), "cols", None),
        P(),
        P(),
    )
    out_specs = (P(("video", "rows"), "cols", None), P(("video", "rows"), "cols", None))
    return jax.shard_map(body, mesh=mesh, in_specs=in_specs, out_specs=out_specs, check_vma=False)
```

time: 102 us -> 62.2 us (0.61)
  Pallas kernels: 0 us -> 28.1 us
  local copies, waits for them, and re-layouts: 34.8 us -> 7.52 us
  matrix products: 14.7 us -> 0 us
  between operations: 14.7 us -> 0.75 us
  other arithmetic: 5.83 us -> 0 us
  waiting for transfers between devices: 10.8 us -> 5.44 us
    pallas_call x0 -> x8, Pallas kernels: none -> 28.1 us  [the longest x3 12.3 us: fold(): pl.pallas_call(functools.partial(fold_kernel, len(blocks), first), in_spe...]
    unnamed x41 -> x26, local copies, waits for them, and re-layouts: 22.5 us -> 3.57 us
    dot_general x5 -> x0, matrix products: 14.7 us -> none  [the longest x1 5.69 us: body(): jnp.dot(patches, kernel_rows, preferred_element_type=jnp.float32)]
    slice x23 -> x0, local copies, waits for them, and re-layouts: 7.18 us -> none  [the longest x20 5.93 us: body(): padded[time_off, row_off:row_off + tile_rows, col_off:col_off + tile_cols...]
    all_gather x1 -> x0, waiting for transfers between devices: 6.41 us -> none  [body(): lax.all_gather(normed, ('rows', 'cols'), axis=0, tiled=True)]
    squeeze x0 -> x4, local copies, waits for them, and re-layouts: none -> 3.96 us  [the longest x1 1.36 us: body(): bottom[2]]
    concatenate x29 -> x0, local copies, waits for them, and re-layouts: 3.75 us -> none  [the longest x27 3.61 us: body(): patches = jnp.concatenate(windows, axis=-1).reshape(count, 27 * channels)]
    concatenate x4 -> x0, other arithmetic: 1.76 us -> none  [padded_2(): value = jnp.concatenate([before, value, after], axis=dim)]
  transfers between devices with their start and end apart: 9 -> 14, of which waited for: 2 -> 3; matrix products, arithmetic and copies ran while one was open for 30% -> 6% of each run, Pallas kernels for 0% -> 28%
where the time goes in v1:
time: 62.2 us; the launch traced here: 61.6 us
  Pallas kernels  28.1 us (45%)
  starting transfers between devices  19.8 us (32%)
  local copies, waits for them, and re-layouts  7.52 us (12%)
  waiting for transfers between devices  5.44 us (9%)
  between operations  0.75 us (1%)
    pallas_call x3, Pallas kernels, fold(): pl.pallas_call(functools.partial(fold_kernel, len(blocks), first), in_spe...  12.3 us
    ppermute x4, starting transfers between devices, body(): chain_a = lax.ppermute(chain_a, AXES, ring)  6.23 us
    ppermute x1, starting transfers between devices, body(): top = lax.ppermute(last, AXES, down)  4.95 us
    ppermute x3, starting transfers between devices, body(): chain_b = lax.ppermute(chain_b, AXES, ring)  4.78 us
    pallas_call x1, Pallas kernels, finish(): pl.pallas_call(functools.partial(finish_kernel, height), in_specs=[VM] *...  4.76 us
    pallas_call x1, Pallas kernels, cache_conv(): pl.pallas_call(cache_conv_kernel, grid=(3,), in_specs=[whole(cache.shape)...  4.68 us
    ppermute x1, waiting for transfers between devices, body(): bottom = lax.ppermute(first, AXES, up)  3.69 us
    unnamed x26, local copies, waits for them, and re-layouts  3.57 us
  transfers between devices with their start and end apart: 14, of which 3 were waited for; matrix products, arithmetic and copies ran while one was open for 6% of the time, Pallas kernels for 28%

profile of v1, /device:TPU:0, one launch (start us, length us, event | category | flops | bytes accessed | tf_op | source)
XLA Modules:
  0.0 61.6 jit_solution(6448705514081194335)
XLA Ops:
  0.6 1.9 %pack_rows.1 = (bf16[3,32,512]{2,1,0:T(8,128)(2,1)}, bf16[3,32,512]{2,1,0:T(8,128)(2,1)}) custom-call(bf16[20,8,512]{2,1,0:T(8,128)(2,1)} %bitcast.24, bf16[2,20,8,512]{3,2,1,0:T(8,128)(2,1)} %bitcast.21), custom_call_target="tpu_custom_call" | custom-call | tf_op jit(solution)/shard_map/pack_rows/pallas_call | solution.py:368
  2.5 4.9 %collective-permute-start = (bf16[3,32,512]{2,1,0:T(8,128)(2,1)}, bf16[3,32,512]{2,1,0:T(8,128)(2,1)S(1)}, u32[]{:S(2)}, u32[]{:S(2)}) collective-permute-start(bf16[3,32,512]{2,1,0:T(8,128)(2,1)} %get-tuple-element.16), channel_id=1, source_target_pairs={{0,4},{1,5},{2,6},{3,7},{4,8},{5,9},{6,10},{7,11},{8,12},{9,13},{1... | collective-permute-start | bytes 294920 | tf_op jit(solution)/shard_map/ppermute | solution.py:371
  7.5 1.3 %collective-permute-start.1 = (bf16[3,32,512]{2,1,0:T(8,128)(2,1)}, bf16[3,32,512]{2,1,0:T(8,128)(2,1)S(1)}, u32[]{:S(2)}, u32[]{:S(2)}) collective-permute-start(bf16[3,32,512]{2,1,0:T(8,128)(2,1)} %get-tuple-element.17), channel_id=1, source_target_pairs={{4,0},{5,1},{6,2},{7,3},{8,4},{9,5},{10,6},{11,7},{12,8},{13,9},{1... | collective-permute-start | bytes 294920 | tf_op jit(solution)/shard_map/ppermute | solution.py:372
  8.8 0.1 collective-permute-start.9
  8.8 2.7 %collective-permute-start.5 = (bf16[160,512]{1,0:T(8,128)(2,1)}, bf16[160,512]{1,0:T(8,128)(2,1)S(1)}, u32[]{:S(2)}, u32[]{:S(2)}) collective-permute-start(bf16[160,512]{1,0:T(8,128)(2,1)} %bitcast.26), channel_id=1, source_target_pairs={{4,8},{9,5},{8,12},{13,9},{12,14},{15,13},{14,10},{11,15},{10,6},{... | collective-permute-start | bytes 491528 | tf_op jit(solution)/shard_map/ppermute | solution.py:360
  11.5 0.0 collective-permute-done.top_ref
  11.5 0.0 copy-start.2
  11.5 3.7 %collective-permute-done.1.bottom_ref = bf16[3,32,512]{2,1,0:T(8,128)(2,1)S(1)} collective-permute-done((bf16[3,32,512]{2,1,0:T(8,128)(2,1)}, bf16[3,32,512]{2,1,0:T(8,128)(2,1)S(1)}, u32[]{:S(2)}, u32[]{:S(2)}) %collective-permute-start.1) | collective-permute-done | bytes 98336 | tf_op jit(solution)/shard_map/ppermute | solution.py:372
  15.2 0.0 copy-done.2
  15.2 0.0 copy-start.3
  15.2 0.6 %copy-done.3 = bf16[3,32,512]{2,1,0:T(8,128)(2,1)} copy-done((bf16[3,32,512]{2,1,0:T(8,128)(2,1)}, bf16[3,32,512]{2,1,0:T(8,128)(2,1)S(1)}, u32[]{:S(2)}) %copy-start.3) | copy-done | bytes 98328
  15.9 1.8 %pack_cols.1 = (bf16[3,16,512]{2,1,0:T(8,128)(2,1)}, bf16[3,16,512]{2,1,0:T(8,128)(2,1)}) custom-call(bf16[20,8,512]{2,1,0:T(8,128)(2,1)} %bitcast.27, bf16[2,20,8,512]{3,2,1,0:T(8,128)(2,1)} %bitcast.22, bf16[3,32,512]{2,1,0:T(8,128)(2,1)} %copy-done.2, bf16[3,32,512]{2,1,0:T(8,128)(2,1)} %copy-done.3), custom_call_target="tpu_custom_call" | custom-call | tf_op jit(solution)/shard_map/pack_cols/pallas_call | solution.py:374
  17.7 0.7 %collective-permute-start.3 = (bf16[3,16,512]{2,1,0:T(8,128)(2,1)}, bf16[3,16,512]{2,1,0:T(8,128)(2,1)S(1)}, u32[]{:S(2)}, u32[]{:S(2)}) collective-permute-start(bf16[3,16,512]{2,1,0:T(8,128)(2,1)} %get-tuple-element.19), channel_id=1, source_target_pairs={{1,2},{2,1},{5,6},{6,5},{9,10},{10,9},{13,14},{14,13},{17,18},{18,... | collective-permute-start | bytes 147464 | tf_op jit(solution)/shard_map/ppermute | solution.py:378
  18.3 1.9 %collective-permute-start.2 = (bf16[3,16,512]{2,1,0:T(8,128)(2,1)}, bf16[3,16,512]{2,1,0:T(8,128)(2,1)S(1)}, u32[]{:S(2)}, u32[]{:S(2)}) collective-permute-start(bf16[3,16,512]{2,1,0:T(8,128)(2,1)} %get-tuple-element.18), channel_id=1, source_target_pairs={{0,1},{1,0},{2,3},{3,2},{4,5},{5,4},{6,7},{7,6},{8,9},{9,8},{10,11... | collective-permute-start | bytes 147464 | tf_op jit(solution)/shard_map/ppermute | solution.py:377
  20.2 1.4 %slice_bitcast_fusion.bottom_ref = bf16[32,512]{1,0:T(8,128)(2,1)} fusion(bf16[3,32,512]{2,1,0:T(8,128)(2,1)} %copy-done.3), kind=kLoop, calls=%fused_computation | loop fusion | bytes 65536 | tf_op jit(solution)/shard_map/squeeze | solution.py:384
  21.6 1.4 %slice_bitcast_fusion.1.top_ref = bf16[32,512]{1,0:T(8,128)(2,1)} fusion(bf16[3,32,512]{2,1,0:T(8,128)(2,1)} %copy-done.2), kind=kLoop, calls=%fused_computation.1 | loop fusion | bytes 65536 | tf_op jit(solution)/shard_map/squeeze | solution.py:384
  22.9 0.0 collective-permute-done.9
  22.9 1.6 %collective-permute-start.10 = (bf16[160,512]{1,0:T(8,128)(2,1)S(1)}, bf16[160,512]{1,0:T(8,128)(2,1)S(1)}, u32[]{:S(2)}, u32[]{:S(2)}) collective-permute-start(bf16[160,512]{1,0:T(8,128)(2,1)S(1)} %collective-permute-done.9), channel_id=1, source_target_pairs={{4,8},{9,5},{8,12},{13,9},{12,14},{15,13},{14,10},{11,15},{10,6},{... | collective-permute-start | bytes 491528 | tf_op jit(solution)/shard_map/ppermute | solution.py:363
  24.5 0.0 collective-permute-done.5.refs_4_
  24.5 0.0 copy-start.5
  24.5 1.6 %collective-permute-start.6 = (bf16[160,512]{1,0:T(8,128)(2,1)S(1)}, bf16[160,512]{1,0:T(8,128)(2,1)S(1)}, u32[]{:S(2)}, u32[]{:S(2)}) collective-permute-start(bf16[160,512]{1,0:T(8,128)(2,1)S(1)} %collective-permute-done.5.refs_4_), channel_id=1, source_target_pairs={{4,8},{9,5},{8,12},{13,9},{12,14},{15,13},{14,10},{11,15},{10,6},{... | collective-permute-start | bytes 491528 | tf_op jit(solution)/shard_map/ppermute | solution.py:360
  26.1 0.0 collective-permute-done.3.cross_ref
  26.1 0.0 copy-start.11
  26.1 0.6 slice_bitcast_fusion.2.cross_ref
  26.7 1.5 %collective-permute-done.10.refs_5_ = bf16[160,512]{1,0:T(8,128)(2,1)S(1)} collective-permute-done((bf16[160,512]{1,0:T(8,128)(2,1)S(1)}, bf16[160,512]{1,0:T(8,128)(2,1)S(1)}, u32[]{:S(2)}, u32[]{:S(2)}) %collective-permute-start.10) | collective-permute-done | bytes 163872 | tf_op jit(solution)/shard_map/ppermute | solution.py:363
  28.2 0.0 copy-start.6
  28.2 1.6 %collective-permute-start.11 = (bf16[160,512]{1,0:T(8,128)(2,1)S(1)}, bf16[160,512]{1,0:T(8,128)(2,1)S(1)}, u32[]{:S(2)}, u32[]{:S(2)}) collective-permute-start(bf16[160,512]{1,0:T(8,128)(2,1)S(1)} %collective-permute-done.10.refs_5_), channel_id=1, source_target_pairs={{4,8},{9,5},{8,12},{13,9},{12,14},{15,13},{14,10},{11,15},{10,6},{... | collective-permute-start | bytes 491528 | tf_op jit(solution)/shard_map/ppermute | solution.py:363
  29.8 0.2 collective-permute-done.6.refs_6_
  30.0 0.0 copy-start.7
  30.0 1.6 %collective-permute-start.7 = (bf16[160,512]{1,0:T(8,128)(2,1)S(1)}, bf16[160,512]{1,0:T(8,128)(2,1)S(1)}, u32[]{:S(2)}, u32[]{:S(2)}) collective-permute-start(bf16[160,512]{1,0:T(8,128)(2,1)S(1)} %collective-permute-done.6.refs_6_), channel_id=1, source_target_pairs={{4,8},{9,5},{8,12},{13,9},{12,14},{15,13},{14,10},{11,15},{10,6},{... | collective-permute-start | bytes 491528 | tf_op jit(solution)/shard_map/ppermute | solution.py:360
  31.6 0.0 collective-permute-done.2.twin_ref
  31.6 0.6 %slice_bitcast_fusion.3.twin_ref = bf16[16,512]{1,0:T(8,128)(2,1)} fusion(bf16[3,16,512]{2,1,0:T(8,128)(2,1)S(1)} %collective-permute-done.2.twin_ref), kind=kLoop, calls=%fused_computation.3 | loop fusion | bytes 32768 | tf_op jit(solution)/shard_map/squeeze | solution.py:384
  32.2 2.7 %query.1 = (bf16[240,512]{1,0:T(8,128)(2,1)}, bf16[240,512]{1,0:T(8,128)(2,1)}) custom-call(bf16[20,8,512]{2,1,0:T(8,128)(2,1)} %bitcast.28, bf16[32,512]{1,0:T(8,128)(2,1)} %slice_bitcast_fusion.1.top_ref, bf16[32,512]{1,0:T(8,128)(2,1)} %slice_bitcast_fusion.bottom_ref, bf16[16,512]{1,0:T(8,128)(2,1)} %slice_bitcast_fusion.3.twin_ref, ...), custom_call_target="tpu_custom_call" | custom-call | tf_op jit(solution)/shard_map/query/pallas_call | solution.py:382
  34.9 0.0 collective-permute-start.4
  34.9 0.0 collective-permute-done.11.refs_7_
  34.9 0.0 copy-start.8
  34.9 1.6 %collective-permute-start.12 = (bf16[160,512]{1,0:T(8,128)(2,1)S(1)}, bf16[160,512]{1,0:T(8,128)(2,1)S(1)}, u32[]{:S(2)}, u32[]{:S(2)}) collective-permute-start(bf16[160,512]{1,0:T(8,128)(2,1)S(1)} %collective-permute-done.11.refs_7_), channel_id=1, source_target_pairs={{4,8},{9,5},{8,12},{13,9},{12,14},{15,13},{14,10},{11,15},{10,6},{... | collective-permute-start | bytes 491528 | tf_op jit(solution)/shard_map/ppermute | solution.py:363
  36.5 0.0 collective-permute-done.7.refs_3_
  36.5 0.0 copy-start.9
  36.5 0.4 collective-permute-start.8
  36.9 0.0 collective-permute-done.4.refs_2_
  36.9 0.0 copy-done.5
  36.9 0.0 copy-done.6
  36.9 0.0 copy-done.7
  36.9 0.0 copy-done.8
  36.9 0.0 copy-start
  36.9 0.7 %copy-done = bf16[240,512]{1,0:T(8,128)(2,1)} copy-done((bf16[240,512]{1,0:T(8,128)(2,1)}, bf16[240,512]{1,0:T(8,128)(2,1)S(1)}, u32[]{:S(2)}) %copy-start) | copy-done | bytes 245784
  37.6 4.1 %fold.3 = (f32[240,768]{1,0:T(8,128)}, f32[240,768]{1,0:T(8,128)}) custom-call(f32[1,512]{1,0:T(1,128)} %bitcast.31, bf16[240,512]{1,0:T(8,128)(2,1)} %get-tuple-element.20.refs_1_, bf16[240,512]{1,0:T(8,128)(2,1)} %copy-done, bf16[160,512]{1,0:T(8,128)(2,1)} %bitcast.29, bf16[160,512]{1,0:T(8,128)(2,1)} %copy-done.5, bf16[160,512]{1,0:T(8,128)(2,1)} %copy-done.6, ...), custom_call_target="tpu_custom_call" | custom-call | tf_op jit(solution)/shard_map/fold/pallas_call | solution.py:265
  41.7 0.0 collective-permute-done.12.refs_4_
  41.7 0.0 copy-start.10
  41.7 0.0 copy-done.9
  41.7 0.6 %copy-done.10 = bf16[160,512]{1,0:T(8,128)(2,1)} copy-done((bf16[160,512]{1,0:T(8,128)(2,1)}, bf16[160,512]{1,0:T(8,128)(2,1)S(1)}, u32[]{:S(2)}) %copy-start.10) | copy-done | bytes 163864
  42.4 4.1 %fold.4 = (f32[240,768]{1,0:T(8,128)}, f32[240,768]{1,0:T(8,128)}) custom-call(f32[1,512]{1,0:T(1,128)} %bitcast.32, bf16[240,512]{1,0:T(8,128)(2,1)} %get-tuple-element.20.refs_1_, bf16[240,512]{1,0:T(8,128)(2,1)} %copy-done, bf16[160,512]{1,0:T(8,128)(2,1)} %copy-done.9, bf16[160,512]{1,0:T(8,128)(2,1)} %copy-done.10, ...), custom_call_target="tpu_custom_call" | custom-call | tf_op jit(solution)/shard_map/fold/pallas_call | solution.py:265
  46.5 0.0 collective-permute-done.8.refs_3_
  46.5 0.0 copy-start.4
  46.5 0.7 %copy-done.4 = bf16[160,512]{1,0:T(8,128)(2,1)} copy-done((bf16[160,512]{1,0:T(8,128)(2,1)}, bf16[160,512]{1,0:T(8,128)(2,1)S(1)}, u32[]{:S(2)}) %copy-start.4) | copy-done | bytes 163864
  47.2 4.1 %fold.5 = (f32[240,768]{1,0:T(8,128)}, f32[240,768]{1,0:T(8,128)}) custom-call(f32[1,512]{1,0:T(1,128)} %bitcast.33, bf16[240,512]{1,0:T(8,128)(2,1)} %get-tuple-element.20.refs_1_, bf16[240,512]{1,0:T(8,128)(2,1)} %copy-done, bf16[160,512]{1,0:T(8,128)(2,1)} %copy-done.4, f32[240,768]{1,0:T(8,128)} %get-tuple-element.23.refs_4_, ...), custom_call_target="tpu_custom_call" | custom-call | tf_op jit(solution)/shard_map/fold/pallas_call | solution.py:265
  51.3 0.0 collective-permute-start.13
  51.3 0.0 copy-done.11
  51.3 0.0 copy-done.12
  51.3 4.7 %cache_conv.1.partial_ref = f32[160,256]{1,0:T(8,128)} custom-call(bf16[2,20,8,512]{3,2,1,0:T(8,128)(2,1)} %bitcast.23, bf16[3,32,512]{2,1,0:T(8,128)(2,1)} %copy-done.2, bf16[3,32,512]{2,1,0:T(8,128)(2,1)} %copy-done.3, bf16[3,16,512]{2,1,0:T(8,128)(2,1)} %copy-done.12, bf16[3,16,512]{2,1,0:T(8,128)(2,1)} %copy-done.11, bf16[3,3,3,512,256]{4,3,2,1,0:T(8,128)(2,1)} %w_ref.3), custom_call_target="tpu_custom_call" | custom-call | tf_op jit(solution)/shard_map/cache_conv/pallas_call | solution.py:191
  56.0 0.0 collective-permute-done.13.other_ref
  56.0 0.9 %copy-done.1 = f32[240,768]{1,0:T(8,128)} copy-done((f32[240,768]{1,0:T(8,128)}, f32[240,768]{1,0:T(8,128)S(1)}, u32[]{:S(2)}) %copy-start.1) | copy-done | bytes 737304
  56.9 4.8 %finish.1 = (bf16[160,512]{1,0:T(8,128)(2,1)}, bf16[160,256]{1,0:T(8,128)(2,1)}) custom-call(f32[240,768]{1,0:T(8,128)} %get-tuple-element.25.state_ref, f32[240,768]{1,0:T(8,128)} %copy-done.1, bf16[240,512]{1,0:T(8,128)(2,1)} %get-tuple-element.27.raw_ref, bf16[512,512]{1,0:T(8,128)(2,1)} %wv_ref.1, bf16[512,512]{1,0:T(8,128)(2,1)} %wo_ref.1, ...), custom_call_target="tpu_custom_call" | custom-call | tf_op jit(solution)/shard_map/finish/pallas_call | solution.py:328
  (2 shorter events, 0.0 us)
Async XLA Ops:
  2.5 9.0 %collective-permute-start = (bf16[3,32,512]{2,1,0:T(8,128)(2,1)}, bf16[3,32,512]{2,1,0:T(8,128)(2,1)S(1)}, u32[]{:S(2)}, u32[]{:S(2)}) collective-permute-start(bf16[3,32,512]{2,1,0:T(8,128)(2,1)} %get-tuple-element.16), channel_id=1, source_target_pairs={{0,4},{1,5},{2,6},{3,7},{4,8},{5,9},{6,10},{7,11},{8,12},{9,13},{1... | collective-permute-start | bytes 294920 | tf_op jit(solution)/shard_map/ppermute | solution.py:371
  7.5 7.8 %collective-permute-start.1 = (bf16[3,32,512]{2,1,0:T(8,128)(2,1)}, bf16[3,32,512]{2,1,0:T(8,128)(2,1)S(1)}, u32[]{:S(2)}, u32[]{:S(2)}) collective-permute-start(bf16[3,32,512]{2,1,0:T(8,128)(2,1)} %get-tuple-element.17), channel_id=1, source_target_pairs={{4,0},{5,1},{6,2},{7,3},{8,4},{9,5},{10,6},{11,7},{12,8},{13,9},{1... | collective-permute-start | bytes 294920 | tf_op jit(solution)/shard_map/ppermute | solution.py:372
  8.8 14.1 %collective-permute-start.9 = (bf16[160,512]{1,0:T(8,128)(2,1)}, bf16[160,512]{1,0:T(8,128)(2,1)S(1)}, u32[]{:S(2)}, u32[]{:S(2)}) collective-permute-start(bf16[160,512]{1,0:T(8,128)(2,1)} %bitcast.25), channel_id=1, source_target_pairs={{0,1},{1,0},{2,3},{3,2},{4,5},{5,4},{6,7},{7,6},{8,9},{9,8},{10,11... | collective-permute-start | bytes 491528 | tf_op jit(solution)/shard_map/ppermute | solution.py:356
  8.8 15.6 %collective-permute-start.5 = (bf16[160,512]{1,0:T(8,128)(2,1)}, bf16[160,512]{1,0:T(8,128)(2,1)S(1)}, u32[]{:S(2)}, u32[]{:S(2)}) collective-permute-start(bf16[160,512]{1,0:T(8,128)(2,1)} %bitcast.26), channel_id=1, source_target_pairs={{4,8},{9,5},{8,12},{13,9},{12,14},{15,13},{14,10},{11,15},{10,6},{... | collective-permute-start | bytes 491528 | tf_op jit(solution)/shard_map/ppermute | solution.py:360
  11.5 3.7 %copy-start.2 = (bf16[3,32,512]{2,1,0:T(8,128)(2,1)}, bf16[3,32,512]{2,1,0:T(8,128)(2,1)S(1)}, u32[]{:S(2)}) copy-start(bf16[3,32,512]{2,1,0:T(8,128)(2,1)S(1)} %collective-permute-done.top_ref) | copy-start | bytes 294916
  15.2 0.6 %copy-start.3 = (bf16[3,32,512]{2,1,0:T(8,128)(2,1)}, bf16[3,32,512]{2,1,0:T(8,128)(2,1)S(1)}, u32[]{:S(2)}) copy-start(bf16[3,32,512]{2,1,0:T(8,128)(2,1)S(1)} %collective-permute-done.1.bottom_ref) | copy-start | bytes 294916
  17.7 8.4 %collective-permute-start.3 = (bf16[3,16,512]{2,1,0:T(8,128)(2,1)}, bf16[3,16,512]{2,1,0:T(8,128)(2,1)S(1)}, u32[]{:S(2)}, u32[]{:S(2)}) collective-permute-start(bf16[3,16,512]{2,1,0:T(8,128)(2,1)} %get-tuple-element.19), channel_id=1, source_target_pairs={{1,2},{2,1},{5,6},{6,5},{9,10},{10,9},{13,14},{14,13},{17,18},{18,... | collective-permute-start | bytes 147464 | tf_op jit(solution)/shard_map/ppermute | solution.py:378
  18.3 13.2 %collective-permute-start.2 = (bf16[3,16,512]{2,1,0:T(8,128)(2,1)}, bf16[3,16,512]{2,1,0:T(8,128)(2,1)S(1)}, u32[]{:S(2)}, u32[]{:S(2)}) collective-permute-start(bf16[3,16,512]{2,1,0:T(8,128)(2,1)} %get-tuple-element.18), channel_id=1, source_target_pairs={{0,1},{1,0},{2,3},{3,2},{4,5},{5,4},{6,7},{7,6},{8,9},{9,8},{10,11... | collective-permute-start | bytes 147464 | tf_op jit(solution)/shard_map/ppermute | solution.py:377
  22.9 5.3 %collective-permute-start.10 = (bf16[160,512]{1,0:T(8,128)(2,1)S(1)}, bf16[160,512]{1,0:T(8,128)(2,1)S(1)}, u32[]{:S(2)}, u32[]{:S(2)}) collective-permute-start(bf16[160,512]{1,0:T(8,128)(2,1)S(1)} %collective-permute-done.9), channel_id=1, source_target_pairs={{4,8},{9,5},{8,12},{13,9},{12,14},{15,13},{14,10},{11,15},{10,6},{... | collective-permute-start | bytes 491528 | tf_op jit(solution)/shard_map/ppermute | solution.py:363
  24.5 12.4 %copy-start.5 = (bf16[160,512]{1,0:T(8,128)(2,1)}, bf16[160,512]{1,0:T(8,128)(2,1)S(1)}, u32[]{:S(2)}) copy-start(bf16[160,512]{1,0:T(8,128)(2,1)S(1)} %collective-permute-done.5.refs_4_) | copy-start | bytes 491524
  24.5 5.5 %collective-permute-start.6 = (bf16[160,512]{1,0:T(8,128)(2,1)S(1)}, bf16[160,512]{1,0:T(8,128)(2,1)S(1)}, u32[]{:S(2)}, u32[]{:S(2)}) collective-permute-start(bf16[160,512]{1,0:T(8,128)(2,1)S(1)} %collective-permute-done.5.refs_4_), channel_id=1, source_target_pairs={{4,8},{9,5},{8,12},{13,9},{12,14},{15,13},{14,10},{11,15},{10,6},{... | collective-permute-start | bytes 491528 | tf_op jit(solution)/shard_map/ppermute | solution.py:360
  26.1 25.2 %copy-start.11 = (bf16[3,16,512]{2,1,0:T(8,128)(2,1)}, bf16[3,16,512]{2,1,0:T(8,128)(2,1)S(1)}, u32[]{:S(2)}) copy-start(bf16[3,16,512]{2,1,0:T(8,128)(2,1)S(1)} %collective-permute-done.3.cross_ref) | copy-start | bytes 147460
  28.2 8.7 %copy-start.6 = (bf16[160,512]{1,0:T(8,128)(2,1)}, bf16[160,512]{1,0:T(8,128)(2,1)S(1)}, u32[]{:S(2)}) copy-start(bf16[160,512]{1,0:T(8,128)(2,1)S(1)} %collective-permute-done.10.refs_5_) | copy-start | bytes 491524
  28.2 6.6 %collective-permute-start.11 = (bf16[160,512]{1,0:T(8,128)(2,1)S(1)}, bf16[160,512]{1,0:T(8,128)(2,1)S(1)}, u32[]{:S(2)}, u32[]{:S(2)}) collective-permute-start(bf16[160,512]{1,0:T(8,128)(2,1)S(1)} %collective-permute-done.10.refs_5_), channel_id=1, source_target_pairs={{4,8},{9,5},{8,12},{13,9},{12,14},{15,13},{14,10},{11,15},{10,6},{... | collective-permute-start | bytes 491528 | tf_op jit(solution)/shard_map/ppermute | solution.py:363
  30.0 6.9 %copy-start.7 = (bf16[160,512]{1,0:T(8,128)(2,1)}, bf16[160,512]{1,0:T(8,128)(2,1)S(1)}, u32[]{:S(2)}) copy-start(bf16[160,512]{1,0:T(8,128)(2,1)S(1)} %collective-permute-done.6.refs_6_) | copy-start | bytes 491524
  30.0 6.5 %collective-permute-start.7 = (bf16[160,512]{1,0:T(8,128)(2,1)S(1)}, bf16[160,512]{1,0:T(8,128)(2,1)S(1)}, u32[]{:S(2)}, u32[]{:S(2)}) collective-permute-start(bf16[160,512]{1,0:T(8,128)(2,1)S(1)} %collective-permute-done.6.refs_6_), channel_id=1, source_target_pairs={{4,8},{9,5},{8,12},{13,9},{12,14},{15,13},{14,10},{11,15},{10,6},{... | collective-permute-start | bytes 491528 | tf_op jit(solution)/shard_map/ppermute | solution.py:360
  31.6 19.7 %copy-start.12 = (bf16[3,16,512]{2,1,0:T(8,128)(2,1)}, bf16[3,16,512]{2,1,0:T(8,128)(2,1)S(1)}, u32[]{:S(2)}) copy-start(bf16[3,16,512]{2,1,0:T(8,128)(2,1)S(1)} %collective-permute-done.2.twin_ref) | copy-start | bytes 147460
  34.9 2.0 %collective-permute-start.4 = (bf16[240,512]{1,0:T(8,128)(2,1)}, bf16[240,512]{1,0:T(8,128)(2,1)S(1)}, u32[]{:S(2)}, u32[]{:S(2)}) collective-permute-start(bf16[240,512]{1,0:T(8,128)(2,1)} %get-tuple-element.20.refs_1_), channel_id=1, source_target_pairs={{0,1},{1,0},{2,3},{3,2},{4,5},{5,4},{6,7},{7,6},{8,9},{9,8},{10,11... | collective-permute-start | bytes 737288 | tf_op jit(solution)/shard_map/ppermute | solution.py:385
  34.9 2.1 %copy-start.8 = (bf16[160,512]{1,0:T(8,128)(2,1)}, bf16[160,512]{1,0:T(8,128)(2,1)S(1)}, u32[]{:S(2)}) copy-start(bf16[160,512]{1,0:T(8,128)(2,1)S(1)} %collective-permute-done.11.refs_7_) | copy-start | bytes 491524
  34.9 6.9 %collective-permute-start.12 = (bf16[160,512]{1,0:T(8,128)(2,1)S(1)}, bf16[160,512]{1,0:T(8,128)(2,1)S(1)}, u32[]{:S(2)}, u32[]{:S(2)}) collective-permute-start(bf16[160,512]{1,0:T(8,128)(2,1)S(1)} %collective-permute-done.11.refs_7_), channel_id=1, source_target_pairs={{4,8},{9,5},{8,12},{13,9},{12,14},{15,13},{14,10},{11,15},{10,6},{... | collective-permute-start | bytes 491528 | tf_op jit(solution)/shard_map/ppermute | solution.py:363
  36.5 5.2 %copy-start.9 = (bf16[160,512]{1,0:T(8,128)(2,1)}, bf16[160,512]{1,0:T(8,128)(2,1)S(1)}, u32[]{:S(2)}) copy-start(bf16[160,512]{1,0:T(8,128)(2,1)S(1)} %collective-permute-done.7.refs_3_) | copy-start | bytes 491524
  36.5 10.0 %collective-permute-start.8 = (bf16[160,512]{1,0:T(8,128)(2,1)S(1)}, bf16[160,512]{1,0:T(8,128)(2,1)S(1)}, u32[]{:S(2)}, u32[]{:S(2)}) collective-permute-start(bf16[160,512]{1,0:T(8,128)(2,1)S(1)} %collective-permute-done.7.refs_3_), channel_id=1, source_target_pairs={{4,8},{9,5},{8,12},{13,9},{12,14},{15,13},{14,10},{11,15},{10,6},{... | collective-permute-start | bytes 491528 | tf_op jit(solution)/shard_map/ppermute | solution.py:360
  36.9 0.7 %copy-start = (bf16[240,512]{1,0:T(8,128)(2,1)}, bf16[240,512]{1,0:T(8,128)(2,1)S(1)}, u32[]{:S(2)}) copy-start(bf16[240,512]{1,0:T(8,128)(2,1)S(1)} %collective-permute-done.4.refs_2_) | copy-start | bytes 737284
  41.7 0.7 %copy-start.10 = (bf16[160,512]{1,0:T(8,128)(2,1)}, bf16[160,512]{1,0:T(8,128)(2,1)S(1)}, u32[]{:S(2)}) copy-start(bf16[160,512]{1,0:T(8,128)(2,1)S(1)} %collective-permute-done.12.refs_4_) | copy-start | bytes 491524
  46.5 0.7 %copy-start.4 = (bf16[160,512]{1,0:T(8,128)(2,1)}, bf16[160,512]{1,0:T(8,128)(2,1)S(1)}, u32[]{:S(2)}) copy-start(bf16[160,512]{1,0:T(8,128)(2,1)S(1)} %collective-permute-done.8.refs_3_) | copy-start | bytes 491524
  51.3 4.7 %collective-permute-start.13 = (f32[240,768]{1,0:T(8,128)}, f32[240,768]{1,0:T(8,128)S(1)}, u32[]{:S(2)}, u32[]{:S(2)}) collective-permute-start(f32[240,768]{1,0:T(8,128)} %get-tuple-element.26), channel_id=1, source_target_pairs={{0,1},{1,0},{2,3},{3,2},{4,5},{5,4},{6,7},{7,6},{8,9},{9,8},{10,11... | collective-permute-start | bytes 2211848 | tf_op jit(solution)/shard_map/ppermute | solution.py:397
  56.0 0.9 %copy-start.1 = (f32[240,768]{1,0:T(8,128)}, f32[240,768]{1,0:T(8,128)S(1)}, u32[]{:S(2)}) copy-start(f32[240,768]{1,0:T(8,128)S(1)} %collective-permute-done.13.other_ref) | copy-start | bytes 2211844

commit v2 on v1

v2 whole, which is shorter than its diff:
```python
import functools
import math

import jax
import jax.numpy as jnp
from jax import lax
from jax.experimental import pallas as pl
from jax.experimental.pallas import tpu as pltpu
from jax.sharding import PartitionSpec as P


EPS = 1e-06
AXES = ("rows", "cols")
F32 = jnp.float32
BF16 = jnp.bfloat16
VM = pl.BlockSpec(memory_space=pltpu.VMEM)


def near(value):
    return pltpu.with_memory_space_constraint(value, pltpu.VMEM)


def call(kernel, outs, args, limit=16 << 20, far_args=(), far=False, scratch=()):
    return pl.pallas_call(
        kernel,
        in_specs=[VM] * len(args) + [pl.BlockSpec(memory_space=pltpu.HBM)] * len(far_args),
        out_specs=[VM] * len(outs),
        out_shape=[
            jax.ShapeDtypeStruct(shape, dtype) if far else pltpu.VMEM(shape, dtype)
            for shape, dtype in outs
        ],
        scratch_shapes=scratch,
        compiler_params=pltpu.CompilerParams(vmem_limit_bytes=limit),
    )(*[near(a) for a in args], *[pltpu.with_memory_space_constraint(a, pltpu.HBM) for a in far_args])


def buffers(*arrays):
    return [pltpu.VMEM(a.shape, a.dtype) for a in arrays] + [pltpu.SemaphoreType.DMA((len(arrays),))]


def chip_cycle(height, width):
    if width == 1 or height == 1:
        return [(z, x) for z in range(height) for x in range(width)]
    order = []
    for x in range(width):
        inner = range(1, height) if x % 2 == 0 else range(height - 1, 0, -1)
        order += [(z, x) for z in inner]
    return order + [(0, x) for x in range(width - 1, -1, -1)]


def permutations(rows, cols):
    def at(z, x, core):
        return z * cols + 2 * x + core

    walk = chip_cycle(rows, cols // 2)
    ring = []
    for k, here in enumerate(walk):
        there = walk[(k + 1) % len(walk)]
        ring += [(at(*here, 0), at(*there, 0)), (at(*there, 1), at(*here, 1))]
    twin = [(i, i ^ 1) for i in range(rows * cols)]
    down = [(i, i + cols) for i in range((rows - 1) * cols)]
    up = [(j, i) for i, j in down]
    cross = []
    for r in range(rows):
        for c in range(1, cols - 1, 2):
            i = r * cols + c
            cross += [(i, i + 1), (i + 1, i)]
    return len(walk), ring, twin, down, up, cross


def edge_slots(width):
    return -(-(width + 2) // 16) * 16


def edge_rows(width):
    return -(-width // 8) * 8


def side_slots(height):
    return height + 8


def rms_scaled(values, gain):
    mean_sq = jnp.mean(values * values, axis=-1, keepdims=True)
    return values * lax.rsqrt(mean_sq + EPS) * gain


def dot(a, b):
    return jnp.dot(a, b, preferred_element_type=F32)


def dot_t(a, b):
    return lax.dot_general(a, b, (((1,), (1,)), ((), ())), preferred_element_type=F32)


def pack_rows_kernel(frame_hbm, cache_hbm, gain_hbm, frame_ref, cache_ref, gain_ref, first_ref, last_ref, sems):
    copies = [
        pltpu.make_async_copy(frame_hbm, frame_ref, sems.at[0]),
        pltpu.make_async_copy(cache_hbm, cache_ref, sems.at[1]),
        pltpu.make_async_copy(gain_hbm, gain_ref, sems.at[2]),
    ]
    for copy in copies:
        copy.start()
    for copy in copies:
        copy.wait()
    width, height, channels = frame_ref.shape
    fill = jnp.zeros((edge_rows(width) - width, channels), F32)
    for t in range(3):
        tile = (frame_ref[...] if t == 2 else cache_ref[t]).astype(F32)
        for r, out in ((0, first_ref), (height - 1, last_ref)):
            row = jnp.concatenate([tile[c, r : r + 1, :] for c in range(width)] + [fill], axis=0)
            out[t] = row.astype(BF16)


def pack_cols_kernel(frame_ref, cache_ref, top_ref, bottom_ref, twin_ref, cross_ref):
    width, height, channels = frame_ref.shape
    odd = lax.rem(lax.axis_index("cols"), 2)
    fill = jnp.zeros((side_slots(height) - height - 2, channels), F32)
    for t in range(3):
        sides = []
        for c in (0, width - 1):
            own = (frame_ref[c] if t == 2 else cache_ref[t, c]).astype(F32)
            top = top_ref[t].astype(F32)[c : c + 1, :]
            bottom = bottom_ref[t].astype(F32)[c : c + 1, :]
            sides.append(jnp.concatenate([own, top, bottom, fill], axis=0))
        left, right = sides
        twin_ref[t] = jnp.where(odd == 1, left, right).astype(BF16)
        cross_ref[t] = jnp.where(odd == 1, right, left).astype(BF16)


def extended(own, top, bottom, twin, cross, odd):
    height = twin.shape[0] - side_slots(0)
    left = jnp.where(odd == 1, twin, cross)
    right = jnp.where(odd == 1, cross, twin)
    width = own.shape[0] // height
    slots = edge_slots(width)
    slot = lax.broadcasted_iota(jnp.int32, (slots, own.shape[1]), 0)
    fill = jnp.zeros((slots - top.shape[0], own.shape[1]), F32)

    def edge(row, k):
        row = jnp.concatenate([row, fill], axis=0)
        row = jnp.where(slot == width, right[k : k + 1, :], row)
        return jnp.where(slot == slots - 1, left[k : k + 1, :], row)

    return jnp.concatenate(
        [edge(top, height), left[:height], own, right[:height], edge(bottom, height + 1)], axis=0
    )


def conv_rows(ext_len, slots, i):
    return (0 if i == 0 else slots), (ext_len if i == 2 else ext_len - slots)


def add_taps(sums, products, i, j, height, count):
    slots = edge_slots(count // height)
    main = products[slots:] if i == 0 else products
    part = main[j * height : j * height + count]
    edge = None
    if i == 0:
        edge = products[:slots]
    if i == 2:
        edge = products[products.shape[0] - slots :]
    if edge is not None and j != 1:
        edge = pltpu.roll(edge, 1 if j == 0 else slots - 1, 0)
    if sums is None:
        return part, edge
    return sums[0] + part, (None if edge is None else sums[1] + edge)


def shifted_rows(sums, i, height):
    main, edge = sums
    if i == 1:
        return main
    count, out = main.shape
    width = count // height
    tile = main.reshape(width, height, out)
    moved = pltpu.roll(tile, 1 if i == 0 else height - 1, 1)
    row = lax.broadcasted_iota(jnp.int32, (height, out), 0)
    at = 0 if i == 0 else height - 1
    cells = [jnp.where(row == at, edge[c : c + 1, :], moved[c]) for c in range(width)]
    return jnp.concatenate(cells, axis=0)


def cache_conv_kernel(
    cache_ref, top_ref, bottom_ref, twin_ref, cross_ref, w_hbm, out_ref, w_ref, sems
):
    copies = [
        pltpu.make_async_copy(w_hbm.at[pl.ds(0, 2), i], w_ref.at[i], sems.at[i]) for i in range(3)
    ]
    for copy in copies:
        copy.start()
    width, height, channels = cache_ref.shape[1:]
    count = width * height
    odd = lax.rem(lax.axis_index("cols"), 2)
    exts = [
        extended(
            cache_ref[t].reshape(count, channels).astype(F32),
            top_ref[t].astype(F32),
            bottom_ref[t].astype(F32),
            twin_ref[t].astype(F32),
            cross_ref[t].astype(F32),
            odd,
        ).astype(BF16)
        for t in range(2)
    ]
    result = None
    for i in range(3):
        lo, hi = conv_rows(exts[0].shape[0], edge_slots(width), i)
        sums = None
        copies[i].wait()
        for j in range(3):
            products = dot(exts[0][lo:hi], w_ref[i, 0, j]) + dot(exts[1][lo:hi], w_ref[i, 1, j])
            sums = add_taps(sums, products, i, j, height, count)
        value = shifted_rows(sums, i, height)
        result = value if result is None else result + value
    out_ref[...] = result


def query_kernel(
    frame_ref, top_ref, bottom_ref, twin_ref, cross_ref, gain_ref, wq_hbm, wk_hbm, raw_ref, keys_ref,
    wq_ref, wk_ref, sems,
):
    copies = [
        pltpu.make_async_copy(wq_hbm, wq_ref, sems.at[0]),
        pltpu.make_async_copy(wk_hbm, wk_ref, sems.at[1]),
    ]
    for copy in copies:
        copy.start()
    width, height, channels = frame_ref.shape
    odd = lax.rem(lax.axis_index("cols"), 2)
    tokens = extended(
        frame_ref[...].reshape(width * height, channels).astype(F32),
        top_ref[2].astype(F32),
        bottom_ref[2].astype(F32),
        twin_ref[2].astype(F32),
        cross_ref[2].astype(F32),
        odd,
    )
    raw_ref[...] = tokens.astype(BF16)
    normed = rms_scaled(tokens, gain_ref[...]).astype(BF16)
    copies[0].wait()
    rows = (dot(normed, wq_ref[...]) * (1.0 / math.sqrt(channels))).astype(BF16)
    copies[1].wait()
    keys_ref[...] = dot_t(rows, wk_ref[...]).astype(BF16)


def lanes(value, width):
    return jnp.broadcast_to(value, (value.shape[0], width))


def key_rows(refs, gain):
    parts = [
        rms_scaled(ref[...].reshape(-1, gain.shape[1]).astype(F32), gain).astype(BF16) for ref in refs
    ]
    return parts[0] if len(parts) == 1 else jnp.concatenate(parts, axis=0)


def fold_kernel(blocks, first, gain_ref, own_ref, twin_ref, *refs):
    keys = key_rows(refs[:blocks], gain_ref[...])
    states, outs = ((None, None), refs[blocks:]) if first else (refs[blocks:-2], refs[-2:])
    channels = keys.shape[1]
    length = own_ref.shape[0]
    all_scores = dot_t(jnp.concatenate([own_ref[...], twin_ref[...]], axis=0), keys)
    peaks, totals, weights = [], [], []
    for k, state in enumerate(states):
        scores = all_scores[k * length : (k + 1) * length]
        peak = jnp.max(scores, axis=1, keepdims=True)
        if not first:
            peak = jnp.maximum(peak, state[:, channels : channels + 1])
        part = jnp.exp(scores - peak)
        peaks.append(peak)
        totals.append(jnp.sum(part, axis=1, keepdims=True))
        weights.append(part.astype(BF16))
    all_summed = dot(jnp.concatenate(weights, axis=0), keys)
    for k, (state, out) in enumerate(zip(states, outs)):
        summed, total, peak = all_summed[k * length : (k + 1) * length], totals[k], peaks[k]
        if not first:
            fade = jnp.exp(state[:, channels : channels + 1] - peak)
            total = total + fade * state[:, channels + 128 : channels + 129]
            summed = summed + fade * state[:, :channels]
        out[:, :channels] = summed
        out[:, channels : channels + 128] = lanes(peak, 128)
        out[:, channels + 128 :] = lanes(total, 128)


def fold(states, own, twin, gain, blocks):
    length, channels = own.shape
    shape = ((length, channels + 256), F32)
    first = states is None
    args = (gain, own, twin, *blocks, *(() if first else states))
    return call(functools.partial(fold_kernel, len(blocks), first), [shape, shape], args, 24 << 20)


def finish_kernel(
    height, state_ref, other_ref, query_ref, last_ref, swapped_ref, key_gain_ref, raw_ref, partial_ref,
    wv_hbm, wo_hbm, gain_hbm, bias_hbm, w_hbm, hidden_ref, mixed_ref,
    wv_ref, wo_ref, gain_ref, bias_ref, w_ref, sems,
):
    copies = [
        pltpu.make_async_copy(wv_hbm, wv_ref, sems.at[0]),
        pltpu.make_async_copy(wo_hbm, wo_ref, sems.at[1]),
        pltpu.make_async_copy(gain_hbm, gain_ref, sems.at[2]),
        pltpu.make_async_copy(bias_hbm, bias_ref, sems.at[3]),
        pltpu.make_async_copy(w_hbm.at[2], w_ref, sems.at[4]),
    ]
    for copy in copies:
        copy.start()
    length, channels = raw_ref.shape
    count, out = partial_ref.shape
    slots = edge_slots(count // height)
    row = lax.axis_index("rows")
    col = lax.axis_index("cols")
    has_top, has_bottom = row > 0, row < lax.axis_size("rows") - 1
    has_left, has_right = col > 0, col < lax.axis_size("cols") - 1

    keys = key_rows((last_ref, swapped_ref), key_gain_ref[...])
    scores = dot_t(query_ref[...], keys)
    peak_a, peak_b = state_ref[:, channels : channels + 1], other_ref[:, channels : channels + 1]
    peak = jnp.maximum(jnp.maximum(peak_a, peak_b), jnp.max(scores, axis=1, keepdims=True))
    fade_a, fade_b = jnp.exp(peak_a - peak), jnp.exp(peak_b - peak)
    weights = jnp.exp(scores - peak)
    total = jnp.sum(weights, axis=1, keepdims=True)
    total = total + fade_a * state_ref[:, channels + 128 : channels + 129]
    total = total + fade_b * other_ref[:, channels + 128 : channels + 129]
    summed = dot(weights.astype(BF16), keys)
    summed = summed + fade_a * state_ref[:, :channels] + fade_b * other_ref[:, :channels]
    pooled = (summed / total).astype(BF16)
    for copy in copies:
        copy.wait()
    attended = dot(pooled, wv_ref[...]).astype(BF16)
    hidden = (raw_ref[...].astype(F32) + dot(attended, wo_ref[...])).astype(BF16)
    wide = hidden.astype(F32)
    value = rms_scaled(wide, gain_ref[...])
    value = value / (1.0 + jnp.exp(-value))
    slot = lax.broadcasted_iota(jnp.int32, (length, 1), 0)
    main_end = length - slots
    width = count // height
    in_top, in_bottom = slot < slots, slot >= main_end
    in_left = (slot >= slots) & (slot < slots + height)
    in_right = (slot >= main_end - height) & (slot < main_end)
    in_left = in_left | (slot == slots - 1) | (slot == length - 1)
    in_right = in_right | (slot == width) | (slot == main_end + width)
    outside = (in_top & jnp.logical_not(has_top)) | (in_bottom & jnp.logical_not(has_bottom))
    outside = outside | (in_left & jnp.logical_not(has_left)) | (in_right & jnp.logical_not(has_right))
    ext = jnp.where(outside, 0.0, value).astype(BF16)

    own = hidden[slots + height : slots + height + count]
    hidden_ref[...] = own
    result = partial_ref[...] + own[:, :out].astype(F32) + bias_ref[...]
    for i in range(3):
        lo, hi = conv_rows(length, slots, i)
        sums = None
        for j in range(3):
            sums = add_taps(sums, dot(ext[lo:hi], w_ref[i, j]), i, j, height, count)
        result = result + shifted_rows(sums, i, height)
    mixed_ref[...] = result.astype(BF16)


def join_kernel(a_ref, b_ref, out_ref):
    count = b_ref.shape[0]
    out_ref[:count] = a_ref[...].reshape(b_ref.shape)
    out_ref[count:] = b_ref[...]


def moved(value, pairs):
    return lax.ppermute(value, AXES, pairs)


def block(
    frame_in, norm_gain, w_query, w_key, w_value, w_out, conv_gain, conv_cache, w_conv, conv_bias
):
    height, width, channels = frame_in.shape
    out_channels = w_conv.shape[4]
    count = height * width
    chips, ring, twin_pairs, down, up, cross_pairs = permutations(
        lax.axis_size("rows"), lax.axis_size("cols")
    )
    frame_far = jnp.transpose(frame_in, (1, 0, 2))
    cache_far = jnp.transpose(conv_cache, (0, 2, 1, 3))
    gain_far = norm_gain.reshape(1, channels)

    edge = ((3, edge_rows(width), channels), BF16)
    frame, cache, gain, first_rows, last_rows = call(
        pack_rows_kernel,
        [(frame_far.shape, BF16), (cache_far.shape, BF16), (gain_far.shape, F32), edge, edge],
        (),
        far_args=(frame_far, cache_far, gain_far),
        scratch=[pltpu.SemaphoreType.DMA((3,))],
    )

    partner = moved(frame_far.reshape(count, channels), twin_pairs)
    (chain,) = call(join_kernel, [((2 * count, channels), BF16)], (frame, partner))
    blocks = [frame]
    hops = (chips - 1) // 2
    for _ in range(hops):
        chain = moved(chain, ring)
        blocks.append(chain)
    last = moved(chain[:count], ring)
    swapped = moved(last, twin_pairs)

    top = moved(last_rows, down)
    bottom = moved(first_rows, up)
    side = ((3, side_slots(height), channels), BF16)
    to_twin, to_cross = call(pack_cols_kernel, [side, side], (frame, cache, top, bottom))
    twin = moved(to_twin, twin_pairs)
    cross = moved(to_cross, cross_pairs)

    ext = ((2 * edge_slots(width) + (width + 2) * height, channels), BF16)
    raw, queries = call(
        query_kernel, [ext, ext], (frame, top, bottom, twin, cross, gain),
        far_args=(w_query, w_key), scratch=buffers(w_query, w_key),
    )
    twin_queries = moved(queries, twin_pairs)
    (partial,) = call(
        cache_conv_kernel, [((count, out_channels), F32)], (cache, top, bottom, twin, cross),
        far_args=(w_conv,),
        scratch=[
            pltpu.VMEM((3, 2) + w_conv.shape[2:], BF16),
            pltpu.SemaphoreType.DMA((3,)),
        ],
    )
    states = None
    for k in range(0, len(blocks), 4):
        states = fold(states, queries, twin_queries, gain, blocks[k : k + 4])
    other = moved(states[1], twin_pairs)
    far_args = (
        w_value, w_out, conv_gain.reshape(1, channels), conv_bias.reshape(1, out_channels), w_conv
    )
    hidden, mixed = call(
        functools.partial(finish_kernel, height),
        [((count, channels), BF16), ((count, out_channels), BF16)],
        (states[0], other, queries, last, swapped, gain, raw, partial),
        24 << 20,
        far_args,
        True,
        buffers(*far_args[:4], jax.ShapeDtypeStruct(w_conv.shape[1:], BF16)),
    )
    hidden = jnp.transpose(hidden.reshape(width, height, channels), (1, 0, 2))
    mixed = jnp.transpose(mixed.reshape(width, height, out_channels), (1, 0, 2))
    return (hidden, mixed)


def solution(mesh):
    in_specs = (
        P(("video", "rows"), "cols", None),
        P(),
        P(),
        P(),
        P(),
        P(),
        P(),
        P(None, ("video", "rows"), "cols", None),
        P(),
        P(),
    )
    out_specs = (P(("video", "rows"), "cols", None), P(("video", "rows"), "cols", None))
    return jax.shard_map(block, mesh=mesh, in_specs=in_specs, out_specs=out_specs, check_vma=False)
```

time: 62.2 us -> 47.4 us (0.76)
  Pallas kernels: 28.1 us -> 12.4 us
  waiting for transfers between devices: 5.44 us -> 13.7 us
  local copies, waits for them, and re-layouts: 7.52 us -> 0.01 us
    pallas_call x8 -> x7, Pallas kernels: 28.1 us -> 12.4 us  [call(): pl.pallas_call(kernel, in_specs=[VM] * len(args) + [pl.BlockSpec(memory_s...]
    ppermute x14 -> x12, waiting for transfers between devices: 5.44 us -> 13.7 us  [moved(): return lax.ppermute(value, AXES, pairs)]
    squeeze x4 -> x0, local copies, waits for them, and re-layouts: 3.96 us -> none  [the longest x1 1.36 us: body(): bottom[2]]
    unnamed x26 -> x0, local copies, waits for them, and re-layouts: 3.57 us -> none
    ppermute x14 -> x12, starting transfers between devices: 19.8 us -> 20.4 us  [moved(): return lax.ppermute(value, AXES, pairs)]
  transfers between devices with their start and end apart: 14 -> 12, of which waited for: 3 -> 6; matrix products, arithmetic and copies ran while one was open for 6% -> 0% of each run, Pallas kernels for 28% -> 13%
where the time goes in v2:
time: 47.4 us; the launch traced here: 47.2 us
  starting transfers between devices  20.4 us (43%)
  waiting for transfers between devices  13.7 us (29%)
  Pallas kernels  12.4 us (26%)
  between operations  0.73 us (2%)
    ppermute x12, starting transfers between devices, moved(): return lax.ppermute(value, AXES, pairs)  20.4 us
    ppermute x12, waiting for transfers between devices, moved(): return lax.ppermute(value, AXES, pairs)  13.7 us
    pallas_call x7, Pallas kernels, call(): pl.pallas_call(kernel, in_specs=[VM] * len(args) + [pl.BlockSpec(memory_s...  12.4 us
  transfers between devices with their start and end apart: 12, of which 6 were waited for; matrix products, arithmetic and copies ran while one was open for 0% of the time, Pallas kernels for 13%

profile of v2, /device:TPU:0, one launch (start us, length us, event | category | flops | bytes accessed | tf_op | source)
XLA Modules:
  0.0 47.2 jit_solution(7782212602996545114)
XLA Ops:
  0.6 0.6 %collective-permute-start.5 = (bf16[160,512]{1,0:T(8,128)(2,1)}, bf16[160,512]{1,0:T(8,128)(2,1)S(1)}, u32[]{:S(2)}, u32[]{:S(2)}) collective-permute-start(bf16[160,512]{1,0:T(8,128)(2,1)} %bitcast.14), channel_id=1, source_target_pairs={{0,1},{1,0},{2,3},{3,2},{4,5},{5,4},{6,7},{7,6},{8,9},{9,8},{10,11... | collective-permute-start | bytes 491528 | tf_op jit(solution)/shard_map/ppermute | solution.py:366
  1.2 1.3 %shard_map.113 = (bf16[20,8,512]{2,1,0:T(8,128)(2,1)S(1)}, bf16[2,20,8,512]{3,2,1,0:T(8,128)(2,1)S(1)}, f32[1,512]{1,0:T(1,128)S(1)}, bf16[3,24,512]{2,1,0:T(8,128)(2,1)S(1)}, bf16[3,24,512]{2,1,0:T(8,128)(2,1)S(1)}) custom-call(bf16[20,8,512]{2,1,0:T(8,128)(2,1)} %bitcast.15, bf16[2,20,8,512]{3,2,1,0:T(8,128)(2,1)} %bitcast.13, f32[1,512]{1,0:T(1,128)} %bitcast.16), custom_call_target="tpu_custom_call" | custom-call | tf_op jit(solution)/shard_map/pallas_call | solution.py:24
  2.5 0.0 collective-permute-done.5.b_ref
  2.5 2.9 %collective-permute-start.6 = (bf16[320,512]{1,0:T(8,128)(2,1)S(1)}, bf16[320,512]{1,0:T(8,128)(2,1)S(1)}, u32[]{:S(2)}, u32[]{:S(2)}) collective-permute-start(bf16[320,512]{1,0:T(8,128)(2,1)S(1)} %shard_map.116), channel_id=1, source_target_pairs={{4,8},{9,5},{8,12},{13,9},{12,14},{15,13},{14,10},{11,15},{10,6},{... | collective-permute-start | bytes 983048 | tf_op jit(solution)/shard_map/ppermute | solution.py:366
  5.4 5.0 %collective-permute-done.6.refs_1_ = bf16[320,512]{1,0:T(8,128)(2,1)S(1)} collective-permute-done((bf16[320,512]{1,0:T(8,128)(2,1)S(1)}, bf16[320,512]{1,0:T(8,128)(2,1)S(1)}, u32[]{:S(2)}, u32[]{:S(2)}) %collective-permute-start.6) | collective-permute-done | bytes 327712 | tf_op jit(solution)/shard_map/ppermute | solution.py:366
  10.4 2.1 %collective-permute-start.7 = (bf16[320,512]{1,0:T(8,128)(2,1)S(1)}, bf16[320,512]{1,0:T(8,128)(2,1)S(1)}, u32[]{:S(2)}, u32[]{:S(2)}) collective-permute-start(bf16[320,512]{1,0:T(8,128)(2,1)S(1)} %collective-permute-done.6.refs_1_), channel_id=1, source_target_pairs={{4,8},{9,5},{8,12},{13,9},{12,14},{15,13},{14,10},{11,15},{10,6},{... | collective-permute-start | bytes 983048 | tf_op jit(solution)/shard_map/ppermute | solution.py:366
  12.5 3.5 %collective-permute-start = (bf16[3,24,512]{2,1,0:T(8,128)(2,1)S(1)}, bf16[3,24,512]{2,1,0:T(8,128)(2,1)S(1)}, u32[]{:S(2)}, u32[]{:S(2)}) collective-permute-start(bf16[3,24,512]{2,1,0:T(8,128)(2,1)S(1)} %get-tuple-element.17), channel_id=1, source_target_pairs={{0,4},{1,5},{2,6},{3,7},{4,8},{5,9},{6,10},{7,11},{8,12},{9,13},{1... | collective-permute-start | bytes 221192 | tf_op jit(solution)/shard_map/ppermute | solution.py:366
  16.0 1.3 %collective-permute-start.1 = (bf16[3,24,512]{2,1,0:T(8,128)(2,1)S(1)}, bf16[3,24,512]{2,1,0:T(8,128)(2,1)S(1)}, u32[]{:S(2)}, u32[]{:S(2)}) collective-permute-start(bf16[3,24,512]{2,1,0:T(8,128)(2,1)S(1)} %get-tuple-element.18), channel_id=1, source_target_pairs={{4,0},{5,1},{6,2},{7,3},{8,4},{9,5},{10,6},{11,7},{12,8},{13,9},{1... | collective-permute-start | bytes 221192 | tf_op jit(solution)/shard_map/ppermute | solution.py:366
  17.3 0.6 %collective-permute-done.7.refs_2_ = bf16[320,512]{1,0:T(8,128)(2,1)S(1)} collective-permute-done((bf16[320,512]{1,0:T(8,128)(2,1)S(1)}, bf16[320,512]{1,0:T(8,128)(2,1)S(1)}, u32[]{:S(2)}, u32[]{:S(2)}) %collective-permute-start.7) | collective-permute-done | bytes 327712 | tf_op jit(solution)/shard_map/ppermute | solution.py:366
  17.9 2.5 %collective-permute-start.8 = (bf16[320,512]{1,0:T(8,128)(2,1)S(1)}, bf16[320,512]{1,0:T(8,128)(2,1)S(1)}, u32[]{:S(2)}, u32[]{:S(2)}) collective-permute-start(bf16[320,512]{1,0:T(8,128)(2,1)S(1)} %collective-permute-done.7.refs_2_), channel_id=1, source_target_pairs={{4,8},{9,5},{8,12},{13,9},{12,14},{15,13},{14,10},{11,15},{10,6},{... | collective-permute-start | bytes 983048 | tf_op jit(solution)/shard_map/ppermute | solution.py:366
  20.4 0.0 collective-permute-done.top_ref
  20.4 2.6 %collective-permute-done.1.bottom_ref = bf16[3,24,512]{2,1,0:T(8,128)(2,1)S(1)} collective-permute-done((bf16[3,24,512]{2,1,0:T(8,128)(2,1)S(1)}, bf16[3,24,512]{2,1,0:T(8,128)(2,1)S(1)}, u32[]{:S(2)}, u32[]{:S(2)}) %collective-permute-start.1) | collective-permute-done | bytes 73760 | tf_op jit(solution)/shard_map/ppermute | solution.py:366
  23.1 0.1 collective-permute-start.2
  23.1 0.7 %collective-permute-start.3 = (bf16[3,16,512]{2,1,0:T(8,128)(2,1)S(1)}, bf16[3,16,512]{2,1,0:T(8,128)(2,1)S(1)}, u32[]{:S(2)}, u32[]{:S(2)}) collective-permute-start(bf16[3,16,512]{2,1,0:T(8,128)(2,1)S(1)} %get-tuple-element.21), channel_id=1, source_target_pairs={{1,2},{2,1},{5,6},{6,5},{9,10},{10,9},{13,14},{14,13},{17,18},{18,... | collective-permute-start | bytes 147464 | tf_op jit(solution)/shard_map/ppermute | solution.py:366
  23.8 0.5 %collective-permute-done.2.twin_ref = bf16[3,16,512]{2,1,0:T(8,128)(2,1)S(1)} collective-permute-done((bf16[3,16,512]{2,1,0:T(8,128)(2,1)S(1)}, bf16[3,16,512]{2,1,0:T(8,128)(2,1)S(1)}, u32[]{:S(2)}, u32[]{:S(2)}) %collective-permute-start.2) | collective-permute-done | bytes 49184 | tf_op jit(solution)/shard_map/ppermute | solution.py:366
  24.4 0.0 collective-permute-done.3.cross_ref
  24.4 1.7 %shard_map.115 = (bf16[240,512]{1,0:T(8,128)(2,1)S(1)}, bf16[240,512]{1,0:T(8,128)(2,1)S(1)}) custom-call(bf16[20,8,512]{2,1,0:T(8,128)(2,1)S(1)} %get-tuple-element.16.frame_ref.a_ref.refs_0_, bf16[3,24,512]{2,1,0:T(8,128)(2,1)S(1)} %collective-permute-done.top_ref, bf16[3,24,512]{2,1,0:T(8,128)(2,1)S(1)} %collective-permute-done.1.bottom_ref, ...), custom_call_target="tpu_custom_call" | custom-call | tf_op jit(solution)/shard_map/pallas_call | solution.py:24
  26.1 4.7 %collective-permute-start.4 = (bf16[240,512]{1,0:T(8,128)(2,1)S(1)}, bf16[240,512]{1,0:T(8,128)(2,1)S(1)}, u32[]{:S(2)}, u32[]{:S(2)}) collective-permute-start(bf16[240,512]{1,0:T(8,128)(2,1)S(1)} %get-tuple-element.22.own_ref.query_ref), channel_id=1, source_target_pairs={{0,1},{1,0},{2,3},{3,2},{4,5},{5,4},{6,7},{7,6},{8,9},{9,8},{10,11... | collective-permute-start | bytes 737288 | tf_op jit(solution)/shard_map/ppermute | solution.py:366
  30.8 1.1 %collective-permute-done.4.twin_ref = bf16[240,512]{1,0:T(8,128)(2,1)S(1)} collective-permute-done((bf16[240,512]{1,0:T(8,128)(2,1)S(1)}, bf16[240,512]{1,0:T(8,128)(2,1)S(1)}, u32[]{:S(2)}, u32[]{:S(2)}) %collective-permute-start.4) | collective-permute-done | bytes 245792 | tf_op jit(solution)/shard_map/ppermute | solution.py:366
  32.0 0.0 collective-permute-done.8.refs_3_
  32.0 2.0 %shard_map.117 = (f32[240,768]{1,0:T(8,128)S(1)}, f32[240,768]{1,0:T(8,128)S(1)}) custom-call(f32[1,512]{1,0:T(1,128)S(1)} %get-tuple-element.15.gain_ref.key_gain_ref, bf16[240,512]{1,0:T(8,128)(2,1)S(1)} %get-tuple-element.22.own_ref.query_ref, bf16[240,512]{1,0:T(8,128)(2,1)S(1)} %collective-permute-done.4.twin_ref, ...), custom_call_target="tpu_custom_call" | custom-call | tf_op jit(solution)/shard_map/pallas_call | solution.py:24
  33.9 0.4 collective-permute-start.9
  34.4 1.6 %collective-permute-start.10 = (bf16[160,512]{1,0:T(8,128)(2,1)S(1)}, bf16[160,512]{1,0:T(8,128)(2,1)S(1)}, u32[]{:S(2)}, u32[]{:S(2)}) collective-permute-start(bf16[160,512]{1,0:T(8,128)(2,1)S(1)} %slice.4), channel_id=1, source_target_pairs={{4,8},{9,5},{8,12},{13,9},{12,14},{15,13},{14,10},{11,15},{10,6},{... | collective-permute-start | bytes 491528 | tf_op jit(solution)/shard_map/ppermute | solution.py:366
  36.0 3.7 %collective-permute-done.10.last_ref = bf16[160,512]{1,0:T(8,128)(2,1)S(1)} collective-permute-done((bf16[160,512]{1,0:T(8,128)(2,1)S(1)}, bf16[160,512]{1,0:T(8,128)(2,1)S(1)}, u32[]{:S(2)}, u32[]{:S(2)}) %collective-permute-start.10) | collective-permute-done | bytes 163872 | tf_op jit(solution)/shard_map/ppermute | solution.py:366
  39.8 0.0 collective-permute-start.11
  39.8 3.3 %shard_map.118.partial_ref = f32[160,256]{1,0:T(8,128)S(1)} custom-call(bf16[2,20,8,512]{3,2,1,0:T(8,128)(2,1)S(1)} %get-tuple-element.19.cache_ref, bf16[3,24,512]{2,1,0:T(8,128)(2,1)S(1)} %collective-permute-done.top_ref, bf16[3,24,512]{2,1,0:T(8,128)(2,1)S(1)} %collective-permute-done.1.bottom_ref, ...), custom_call_target="tpu_custom_call" | custom-call | tf_op jit(solution)/shard_map/pallas_call | solution.py:24
  43.0 0.0 collective-permute-done.11.swapped_ref
  43.0 0.0 collective-permute-done.9.other_ref
  43.1 4.1 %shard_map.119 = (bf16[160,512]{1,0:T(8,128)(2,1)}, bf16[160,256]{1,0:T(8,128)(2,1)}) custom-call(f32[240,768]{1,0:T(8,128)S(1)} %get-tuple-element.23.state_ref, f32[240,768]{1,0:T(8,128)S(1)} %collective-permute-done.9.other_ref, bf16[240,512]{1,0:T(8,128)(2,1)S(1)} %get-tuple-element.22.own_ref.query_ref, ...), custom_call_target="tpu_custom_call" | custom-call | tf_op jit(solution)/shard_map/pallas_call | solution.py:24
  (3 shorter events, 0.1 us)
Async XLA Ops:
  0.6 1.8 %collective-permute-start.5 = (bf16[160,512]{1,0:T(8,128)(2,1)}, bf16[160,512]{1,0:T(8,128)(2,1)S(1)}, u32[]{:S(2)}, u32[]{:S(2)}) collective-permute-start(bf16[160,512]{1,0:T(8,128)(2,1)} %bitcast.14), channel_id=1, source_target_pairs={{0,1},{1,0},{2,3},{3,2},{4,5},{5,4},{6,7},{7,6},{8,9},{9,8},{10,11... | collective-permute-start | bytes 491528 | tf_op jit(solution)/shard_map/ppermute | solution.py:366
  2.5 7.9 %collective-permute-start.6 = (bf16[320,512]{1,0:T(8,128)(2,1)S(1)}, bf16[320,512]{1,0:T(8,128)(2,1)S(1)}, u32[]{:S(2)}, u32[]{:S(2)}) collective-permute-start(bf16[320,512]{1,0:T(8,128)(2,1)S(1)} %shard_map.116), channel_id=1, source_target_pairs={{4,8},{9,5},{8,12},{13,9},{12,14},{15,13},{14,10},{11,15},{10,6},{... | collective-permute-start | bytes 983048 | tf_op jit(solution)/shard_map/ppermute | solution.py:366
  10.4 7.5 %collective-permute-start.7 = (bf16[320,512]{1,0:T(8,128)(2,1)S(1)}, bf16[320,512]{1,0:T(8,128)(2,1)S(1)}, u32[]{:S(2)}, u32[]{:S(2)}) collective-permute-start(bf16[320,512]{1,0:T(8,128)(2,1)S(1)} %collective-permute-done.6.refs_1_), channel_id=1, source_target_pairs={{4,8},{9,5},{8,12},{13,9},{12,14},{15,13},{14,10},{11,15},{10,6},{... | collective-permute-start | bytes 983048 | tf_op jit(solution)/shard_map/ppermute | solution.py:366
  12.5 7.9 %collective-permute-start = (bf16[3,24,512]{2,1,0:T(8,128)(2,1)S(1)}, bf16[3,24,512]{2,1,0:T(8,128)(2,1)S(1)}, u32[]{:S(2)}, u32[]{:S(2)}) collective-permute-start(bf16[3,24,512]{2,1,0:T(8,128)(2,1)S(1)} %get-tuple-element.17), channel_id=1, source_target_pairs={{0,4},{1,5},{2,6},{3,7},{4,8},{5,9},{6,10},{7,11},{8,12},{9,13},{1... | collective-permute-start | bytes 221192 | tf_op jit(solution)/shard_map/ppermute | solution.py:366
  16.0 7.0 %collective-permute-start.1 = (bf16[3,24,512]{2,1,0:T(8,128)(2,1)S(1)}, bf16[3,24,512]{2,1,0:T(8,128)(2,1)S(1)}, u32[]{:S(2)}, u32[]{:S(2)}) collective-permute-start(bf16[3,24,512]{2,1,0:T(8,128)(2,1)S(1)} %get-tuple-element.18), channel_id=1, source_target_pairs={{4,0},{5,1},{6,2},{7,3},{8,4},{9,5},{10,6},{11,7},{12,8},{13,9},{1... | collective-permute-start | bytes 221192 | tf_op jit(solution)/shard_map/ppermute | solution.py:366
  17.9 14.1 %collective-permute-start.8 = (bf16[320,512]{1,0:T(8,128)(2,1)S(1)}, bf16[320,512]{1,0:T(8,128)(2,1)S(1)}, u32[]{:S(2)}, u32[]{:S(2)}) collective-permute-start(bf16[320,512]{1,0:T(8,128)(2,1)S(1)} %collective-permute-done.7.refs_2_), channel_id=1, source_target_pairs={{4,8},{9,5},{8,12},{13,9},{12,14},{15,13},{14,10},{11,15},{10,6},{... | collective-permute-start | bytes 983048 | tf_op jit(solution)/shard_map/ppermute | solution.py:366
  23.1 1.3 %collective-permute-start.2 = (bf16[3,16,512]{2,1,0:T(8,128)(2,1)S(1)}, bf16[3,16,512]{2,1,0:T(8,128)(2,1)S(1)}, u32[]{:S(2)}, u32[]{:S(2)}) collective-permute-start(bf16[3,16,512]{2,1,0:T(8,128)(2,1)S(1)} %get-tuple-element.20), channel_id=1, source_target_pairs={{0,1},{1,0},{2,3},{3,2},{4,5},{5,4},{6,7},{7,6},{8,9},{9,8},{10,11... | collective-permute-start | bytes 147464 | tf_op jit(solution)/shard_map/ppermute | solution.py:366
  23.1 1.2 %collective-permute-start.3 = (bf16[3,16,512]{2,1,0:T(8,128)(2,1)S(1)}, bf16[3,16,512]{2,1,0:T(8,128)(2,1)S(1)}, u32[]{:S(2)}, u32[]{:S(2)}) collective-permute-start(bf16[3,16,512]{2,1,0:T(8,128)(2,1)S(1)} %get-tuple-element.21), channel_id=1, source_target_pairs={{1,2},{2,1},{5,6},{6,5},{9,10},{10,9},{13,14},{14,13},{17,18},{18,... | collective-permute-start | bytes 147464 | tf_op jit(solution)/shard_map/ppermute | solution.py:366
  26.1 5.9 %collective-permute-start.4 = (bf16[240,512]{1,0:T(8,128)(2,1)S(1)}, bf16[240,512]{1,0:T(8,128)(2,1)S(1)}, u32[]{:S(2)}, u32[]{:S(2)}) collective-permute-start(bf16[240,512]{1,0:T(8,128)(2,1)S(1)} %get-tuple-element.22.own_ref.query_ref), channel_id=1, source_target_pairs={{0,1},{1,0},{2,3},{3,2},{4,5},{5,4},{6,7},{7,6},{8,9},{9,8},{10,11... | collective-permute-start | bytes 737288 | tf_op jit(solution)/shard_map/ppermute | solution.py:366
  33.9 9.1 %collective-permute-start.9 = (f32[240,768]{1,0:T(8,128)S(1)}, f32[240,768]{1,0:T(8,128)S(1)}, u32[]{:S(2)}, u32[]{:S(2)}) collective-permute-start(f32[240,768]{1,0:T(8,128)S(1)} %get-tuple-element.24), channel_id=1, source_target_pairs={{0,1},{1,0},{2,3},{3,2},{4,5},{5,4},{6,7},{7,6},{8,9},{9,8},{10,11... | collective-permute-start | bytes 2211848 | tf_op jit(solution)/shard_map/ppermute | solution.py:366
  34.4 5.4 %collective-permute-start.10 = (bf16[160,512]{1,0:T(8,128)(2,1)S(1)}, bf16[160,512]{1,0:T(8,128)(2,1)S(1)}, u32[]{:S(2)}, u32[]{:S(2)}) collective-permute-start(bf16[160,512]{1,0:T(8,128)(2,1)S(1)} %slice.4), channel_id=1, source_target_pairs={{4,8},{9,5},{8,12},{13,9},{12,14},{15,13},{14,10},{11,15},{10,6},{... | collective-permute-start | bytes 491528 | tf_op jit(solution)/shard_map/ppermute | solution.py:366
  39.8 3.3 %collective-permute-start.11 = (bf16[160,512]{1,0:T(8,128)(2,1)S(1)}, bf16[160,512]{1,0:T(8,128)(2,1)S(1)}, u32[]{:S(2)}, u32[]{:S(2)}) collective-permute-start(bf16[160,512]{1,0:T(8,128)(2,1)S(1)} %collective-permute-done.10.last_ref), channel_id=1, source_target_pairs={{0,1},{1,0},{2,3},{3,2},{4,5},{5,4},{6,7},{7,6},{8,9},{9,8},{10,11... | collective-permute-start | bytes 491528 | tf_op jit(solution)/shard_map/ppermute | solution.py:366
